TPU v7x, 512 devices: a whole 4x8x8 slice. The times are simulated.
512 devices in a mesh: tm: 16 (over y, x_hi), gz: 32 (over x_lo, z, core).
Axes of the slice: x: 4 (x_hi: 2, x_lo: 2; x = x_hi * 2 + x_lo), y: 8, z: 8, core: 2. Of those that a mesh axis runs over, the one named last changes fastest.
Arguments:
- states: float32 [16, 4, 128, 64, 128], P('tm', None, 'gz'), may hold values from -6 to 6
- shift: int32 [1], replicated, may hold values from 0 to 127
- step_size: float32 [1], replicated, may hold values from 0.1 to 0.5
Outputs:
- updated: float32 [16, 4, 128, 64, 128], P('tm', None, 'gz')
- mismatch: float32 [16, 4, 128, 64, 128], P('tm', None, 'gz')
All inputs are finite; a program needn't handle non-finite values.
Results may differ from a plain program's by a relative error of at most 0.00002.
Values sent between devices are 32-bit elements; how exact they have to be, the bound alone decides.
No kernel may reach another device: no remote copies, remote signals or barrier semaphores. Data moves between devices by JAX's collectives and lax.ppermute only.
A program may use at most 64 MiB of HBM per device.

v0:
```python
import jax
import jax.numpy as jnp
from jax import lax
from jax.sharding import PartitionSpec as P

SWEEPS = 3


time_step = 0.2
viscous = 1.0


def with_halo(cells, sides, width):
    for axis, dim in sides:
        count = lax.axis_size(axis)
        head = lax.slice_in_dim(cells, 0, width, axis=dim)
        tail = lax.slice_in_dim(cells, cells.shape[dim] - width, cells.shape[dim], axis=dim)
        cells = jnp.concatenate(
            [
                lax.ppermute(tail, axis, [(i, (i + 1) % count) for i in range(count)]),
                cells,
                lax.ppermute(head, axis, [((i + 1) % count, i) for i in range(count)]),
            ],
            axis=dim,
        )
    return cells


def shifted(block, axis, distance):
    devices = range(lax.axis_size(axis))
    route = [((i - distance) % len(devices), i) for i in devices]
    return lax.ppermute(block, axis, route)


def base_speed(rows):
    radius = 1.0 + (jnp.arange(rows, dtype=jnp.float32) + 0.5) / rows
    return (0.2 + 0.6 / (radius * radius))[:, None]


def radial_pad(centre):
    return jnp.pad(centre, ((0, 0), (0, 0), (1, 1), (0, 0)))


def explicit(padded, flow_speed):
    centre = padded[:, 1:-1]
    along_z = (padded[:, 2:] - padded[:, :-2]) * 0.5
    along_th = (jnp.roll(centre, -1, 3) - jnp.roll(centre, 1, 3)) * 0.5
    walled = radial_pad(centre)
    along_r = (walled[:, :, 2:] - walled[:, :, :-2]) * 0.5
    radial, azimuth, axial, pressure = (centre[0], centre[1], centre[2], centre[3])
    advect = (flow_speed + azimuth) * along_th + radial * along_r + axial * along_z
    new_radial = radial - time_step * (advect[0] - 2.0 * flow_speed * azimuth + along_r[3])
    new_azimuth = azimuth - time_step * (advect[1] + flow_speed * radial + along_th[3])
    new_axial = axial - time_step * (advect[2] + along_z[3])
    new_pressure = pressure - time_step * (along_r[0] + along_th[1] + along_z[2])
    return jnp.stack([new_radial, new_azimuth, new_axial, new_pressure])


def inner_sum(padded):
    centre = padded[:, 1:-1]
    walled = radial_pad(centre)
    total = padded[:, 2:] + padded[:, :-2]
    total = total + jnp.roll(centre, 1, 3) + jnp.roll(centre, -1, 3)
    return total + walled[:, :, 2:] + walled[:, :, :-2]


def neighbour_sum(field):
    padded = with_halo(field, (("gz", 1),), 1)
    return inner_sum(padded)


def return_rims(cotangent):
    rims = jnp.concatenate([cotangent[:, :1], cotangent[:, -1:]], axis=1)
    extended = with_halo(rims, (("gz", 1),), 1)
    inside = cotangent[:, 1:-1]
    lowest = inside[:, :1] + extended[:, :1]
    highest = inside[:, -1:] + extended[:, 3:]
    return jnp.concatenate([lowest, inside[:, 1:-1], highest], axis=1)


def step_adjoint(padded, cotangent, flow_speed):
    scale = 1.0 / (1.0 + 6.0 * viscous)
    force_cot = jnp.zeros_like(cotangent)
    current = cotangent
    for number in range(SWEEPS):
        force_cot = force_cot + current * scale
        current = viscous * scale * neighbour_sum(current)
    force_cot = force_cot + current
    _, puller = jax.vjp(lambda source: explicit(source, flow_speed), padded)
    return return_rims(puller(force_cot)[0])


def per_device(states, shift, step_size):
    start = states[0]
    flow_speed = base_speed(start.shape[2])
    offset = shift[0]
    padded = with_halo(start, (("gz", 1),), 1)
    force = explicit(padded, flow_speed)
    iterate = force
    for level in range(SWEEPS):
        iterate = (force + viscous * neighbour_sum(iterate)) / (1.0 + 6.0 * viscous)
    section_id = lax.axis_index("tm")
    is_first = section_id == 0
    ends = shifted(iterate, "tm", 1)
    target = jnp.where(is_first, jnp.roll(start, offset, axis=3), start)
    earlier = ends - target
    mismatch = shifted(earlier, "tm", -1)
    prior = jnp.where(is_first, jnp.roll(earlier, -offset, axis=3), earlier)
    cotangent = mismatch
    cotangent = step_adjoint(padded, cotangent, flow_speed)
    updated = start - step_size[0] * (cotangent - prior)
    return (updated[None], mismatch[None])


def solution(mesh):
    placed = (P("tm", None, "gz", None, None), P(), P())
    return jax.shard_map(
        per_device,
        mesh=mesh,
        in_specs=placed,
        out_specs=(P("tm", None, "gz", None, None), P("tm", None, "gz", None, None)),
        check_vma=False,
    )
```

profile of v0, /device:TPU:1, one launch (start us, length us, event | category | flops | bytes accessed | tf_op | source)
XLA Modules:
  0.0 132.6 jit_solution(2285658598478369185)
XLA Ops:
  0.6 1.0 fusion.87
  1.7 5.4 %collective-permute-start.1 = (f32[4,1,64,128]{3,2,1,0:T(8,128)S(1)}, f32[4,1,64,128]{3,2,1,0:T(8,128)S(1)}, u32[]{:S(2)}, u32[]{:S(2)}) collective-permute-start(f32[4,1,64,128]{3,2,1,0:T(8,128)S(1)} %get-tuple-element.85), channel_id=1, source_target_pairs={{0,1},{1,2},{2,3},{3,4},{4,5},{5,6},{6,7},{7,8},{8,9},{9,10},{10,1... | collective-permute-start | bytes 393224 | tf_op jit(solution)/shard_map/ppermute | solution.py:20
  7.1 5.3 %collective-permute-start = (f32[4,1,64,128]{3,2,1,0:T(8,128)S(1)}, f32[4,1,64,128]{3,2,1,0:T(8,128)S(1)}, u32[]{:S(2)}, u32[]{:S(2)}) collective-permute-start(f32[4,1,64,128]{3,2,1,0:T(8,128)S(1)} %get-tuple-element.84), channel_id=1, source_target_pairs={{1,0},{2,1},{3,2},{4,3},{5,4},{6,5},{7,6},{8,7},{9,8},{10,9},{11,1... | collective-permute-start | bytes 393224 | tf_op jit(solution)/shard_map/ppermute | solution.py:22
  12.4 0.2 fusion.85
  12.7 0.2 fusion.86
  12.9 0.1 broadcast_multiply_fusion.7
  13.0 0.4 collective-permute-done
  13.4 0.6 multiply_add_fusion
  14.0 0.1 fusion.59
  14.2 0.2 fusion.82
  14.4 1.9 %collective-permute-start.3 = (f32[4,1,64,128]{3,2,1,0:T(8,128)S(1)}, f32[4,1,64,128]{3,2,1,0:T(8,128)S(1)}, u32[]{:S(2)}, u32[]{:S(2)}) collective-permute-start(f32[4,1,64,128]{3,2,1,0:T(8,128)S(1)} %get-tuple-element.76), channel_id=1, source_target_pairs={{0,1},{1,2},{2,3},{3,4},{4,5},{5,6},{6,7},{7,8},{8,9},{9,10},{10,1... | collective-permute-start | bytes 393224 | tf_op jit(solution)/shard_map/ppermute | solution.py:20
  16.4 7.5 %collective-permute-start.2 = (f32[4,1,64,128]{3,2,1,0:T(8,128)S(1)}, f32[4,1,64,128]{3,2,1,0:T(8,128)S(1)}, u32[]{:S(2)}, u32[]{:S(2)}) collective-permute-start(f32[4,1,64,128]{3,2,1,0:T(8,128)S(1)} %get-tuple-element.75), channel_id=1, source_target_pairs={{1,0},{2,1},{3,2},{4,3},{5,4},{6,5},{7,6},{8,7},{9,8},{10,9},{11,1... | collective-permute-start | bytes 393224 | tf_op jit(solution)/shard_map/ppermute | solution.py:22
  23.8 0.2 fusion.83
  24.1 0.7 collective-permute-done.2
  24.8 0.5 fusion.4
  25.4 0.2 fusion.79
  25.6 1.9 %collective-permute-start.5 = (f32[4,1,64,128]{3,2,1,0:T(8,128)S(1)}, f32[4,1,64,128]{3,2,1,0:T(8,128)S(1)}, u32[]{:S(2)}, u32[]{:S(2)}) collective-permute-start(f32[4,1,64,128]{3,2,1,0:T(8,128)S(1)} %get-tuple-element.70), channel_id=1, source_target_pairs={{0,1},{1,2},{2,3},{3,4},{4,5},{5,6},{6,7},{7,8},{8,9},{9,10},{10,1... | collective-permute-start | bytes 393224 | tf_op jit(solution)/shard_map/ppermute | solution.py:20
  27.5 7.4 %collective-permute-start.4 = (f32[4,1,64,128]{3,2,1,0:T(8,128)S(1)}, f32[4,1,64,128]{3,2,1,0:T(8,128)S(1)}, u32[]{:S(2)}, u32[]{:S(2)}) collective-permute-start(f32[4,1,64,128]{3,2,1,0:T(8,128)S(1)} %get-tuple-element.69), channel_id=1, source_target_pairs={{1,0},{2,1},{3,2},{4,3},{5,4},{6,5},{7,6},{8,7},{9,8},{10,9},{11,1... | collective-permute-start | bytes 393224 | tf_op jit(solution)/shard_map/ppermute | solution.py:22
  34.9 0.2 fusion.80
  35.2 0.0 collective-permute-done.5
  35.2 0.7 collective-permute-done.4
  35.9 0.5 fusion.8
  36.4 0.2 fusion.76
  36.6 1.9 %collective-permute-start.7 = (f32[4,1,64,128]{3,2,1,0:T(8,128)S(1)}, f32[4,1,64,128]{3,2,1,0:T(8,128)S(1)}, u32[]{:S(2)}, u32[]{:S(2)}) collective-permute-start(f32[4,1,64,128]{3,2,1,0:T(8,128)S(1)} %get-tuple-element.64), channel_id=1, source_target_pairs={{0,1},{1,2},{2,3},{3,4},{4,5},{5,6},{6,7},{7,8},{8,9},{9,10},{10,1... | collective-permute-start | bytes 393224 | tf_op jit(solution)/shard_map/ppermute | solution.py:20
  38.6 7.4 %collective-permute-start.6 = (f32[4,1,64,128]{3,2,1,0:T(8,128)S(1)}, f32[4,1,64,128]{3,2,1,0:T(8,128)S(1)}, u32[]{:S(2)}, u32[]{:S(2)}) collective-permute-start(f32[4,1,64,128]{3,2,1,0:T(8,128)S(1)} %get-tuple-element.63), channel_id=1, source_target_pairs={{1,0},{2,1},{3,2},{4,3},{5,4},{6,5},{7,6},{8,7},{9,8},{10,9},{11,1... | collective-permute-start | bytes 393224 | tf_op jit(solution)/shard_map/ppermute | solution.py:22
  46.0 0.2 fusion.77
  46.2 0.7 collective-permute-done.6
  47.0 0.5 fusion.12
  47.5 4.4 %collective-permute-start.8 = (f32[4,4,64,128]{3,2,1,0:T(8,128)S(1)}, f32[4,4,64,128]{3,2,1,0:T(8,128)S(1)}, u32[]{:S(2)}, u32[]{:S(2)}) collective-permute-start(f32[4,4,64,128]{3,2,1,0:T(8,128)S(1)} %fusion.12), channel_id=1, source_target_pairs={{480,0},{0,32},{32,64},{64,96},{96,128},{128,160},{160,192},{192,2... | collective-permute-start | bytes 1572872 | tf_op jit(solution)/shard_map/ppermute | solution.py:32
  52.5 8.8 %collective-permute-done.8 = f32[4,4,64,128]{3,2,1,0:T(8,128)S(1)} collective-permute-done((f32[4,4,64,128]{3,2,1,0:T(8,128)S(1)}, f32[4,4,64,128]{3,2,1,0:T(8,128)S(1)}, u32[]{:S(2)}, u32[]{:S(2)}) %collective-permute-start.8) | collective-permute-done | bytes 524320 | tf_op jit(solution)/shard_map/ppermute | solution.py:32
  61.3 0.3 fusion.29
  61.6 4.9 %collective-permute-start.9 = (f32[4,4,64,128]{3,2,1,0:T(8,128)S(1)}, f32[4,4,64,128]{3,2,1,0:T(8,128)S(1)}, u32[]{:S(2)}, u32[]{:S(2)}) collective-permute-start(f32[4,4,64,128]{3,2,1,0:T(8,128)S(1)} %fusion.29), channel_id=1, source_target_pairs={{32,0},{64,32},{96,64},{128,96},{160,128},{192,160},{224,192},{256... | collective-permute-start | bytes 1572872 | tf_op jit(solution)/shard_map/ppermute | solution.py:32
  66.6 6.5 %collective-permute-done.9 = f32[4,4,64,128]{3,2,1,0:T(8,128)S(1)} collective-permute-done((f32[4,4,64,128]{3,2,1,0:T(8,128)S(1)}, f32[4,4,64,128]{3,2,1,0:T(8,128)S(1)}, u32[]{:S(2)}, u32[]{:S(2)}) %collective-permute-start.9) | collective-permute-done | bytes 524320 | tf_op jit(solution)/shard_map/ppermute | solution.py:32
  73.1 9.9 %collective-permute-start.11 = (f32[4,1,64,128]{3,2,1,0:T(8,128)S(1)}, f32[4,1,64,128]{3,2,1,0:T(8,128)S(1)}, u32[]{:S(2)}, u32[]{:S(2)}) collective-permute-start(f32[4,1,64,128]{3,2,1,0:T(8,128)S(1)} %get-tuple-element.54), channel_id=1, source_target_pairs={{0,1},{1,2},{2,3},{3,4},{4,5},{5,6},{6,7},{7,8},{8,9},{9,10},{10,1... | collective-permute-start | bytes 393224 | tf_op jit(solution)/shard_map/ppermute | solution.py:20
  83.0 1.9 %collective-permute-start.10 = (f32[4,1,64,128]{3,2,1,0:T(8,128)S(1)}, f32[4,1,64,128]{3,2,1,0:T(8,128)S(1)}, u32[]{:S(2)}, u32[]{:S(2)}) collective-permute-start(f32[4,1,64,128]{3,2,1,0:T(8,128)S(1)} %get-tuple-element.53), channel_id=1, source_target_pairs={{1,0},{2,1},{3,2},{4,3},{5,4},{6,5},{7,6},{8,7},{9,8},{10,9},{11,1... | collective-permute-start | bytes 393224 | tf_op jit(solution)/shard_map/ppermute | solution.py:22
  85.0 0.2 fusion.74
  85.2 0.2 fusion.75
  85.4 3.9 %collective-permute-done.10 = f32[4,1,64,128]{3,2,1,0:T(8,128)S(1)} collective-permute-done((f32[4,1,64,128]{3,2,1,0:T(8,128)S(1)}, f32[4,1,64,128]{3,2,1,0:T(8,128)S(1)}, u32[]{:S(2)}, u32[]{:S(2)}) %collective-permute-start.10) | collective-permute-done | bytes 131104 | tf_op jit(solution)/shard_map/ppermute | solution.py:22
  89.3 0.5 broadcast_multiply_fusion.1
  89.8 0.2 fusion.71
  90.0 1.9 %collective-permute-start.13 = (f32[4,1,64,128]{3,2,1,0:T(8,128)S(1)}, f32[4,1,64,128]{3,2,1,0:T(8,128)S(1)}, u32[]{:S(2)}, u32[]{:S(2)}) collective-permute-start(f32[4,1,64,128]{3,2,1,0:T(8,128)S(1)} %get-tuple-element.48), channel_id=1, source_target_pairs={{0,1},{1,2},{2,3},{3,4},{4,5},{5,6},{6,7},{7,8},{8,9},{9,10},{10,1... | collective-permute-start | bytes 393224 | tf_op jit(solution)/shard_map/ppermute | solution.py:20
  92.0 7.5 %collective-permute-start.12 = (f32[4,1,64,128]{3,2,1,0:T(8,128)S(1)}, f32[4,1,64,128]{3,2,1,0:T(8,128)S(1)}, u32[]{:S(2)}, u32[]{:S(2)}) collective-permute-start(f32[4,1,64,128]{3,2,1,0:T(8,128)S(1)} %get-tuple-element.47), channel_id=1, source_target_pairs={{1,0},{2,1},{3,2},{4,3},{5,4},{6,5},{7,6},{8,7},{9,8},{10,9},{11,1... | collective-permute-start | bytes 393224 | tf_op jit(solution)/shard_map/ppermute | solution.py:22
  99.5 0.2 fusion.72
  99.7 0.7 collective-permute-done.12
  100.5 0.5 broadcast_multiply_fusion
  101.0 0.2 fusion.67
  101.2 1.9 %collective-permute-start.15 = (f32[4,1,64,128]{3,2,1,0:T(8,128)S(1)}, f32[4,1,64,128]{3,2,1,0:T(8,128)S(1)}, u32[]{:S(2)}, u32[]{:S(2)}) collective-permute-start(f32[4,1,64,128]{3,2,1,0:T(8,128)S(1)} %get-tuple-element.46), channel_id=1, source_target_pairs={{0,1},{1,2},{2,3},{3,4},{4,5},{5,6},{6,7},{7,8},{8,9},{9,10},{10,1... | collective-permute-start | bytes 393224 | tf_op jit(solution)/shard_map/ppermute | solution.py:20
  103.1 7.4 %collective-permute-start.14 = (f32[4,1,64,128]{3,2,1,0:T(8,128)S(1)}, f32[4,1,64,128]{3,2,1,0:T(8,128)S(1)}, u32[]{:S(2)}, u32[]{:S(2)}) collective-permute-start(f32[4,1,64,128]{3,2,1,0:T(8,128)S(1)} %get-tuple-element.45), channel_id=1, source_target_pairs={{1,0},{2,1},{3,2},{4,3},{5,4},{6,5},{7,6},{8,7},{9,8},{10,9},{11,1... | collective-permute-start | bytes 393224 | tf_op jit(solution)/shard_map/ppermute | solution.py:22
  110.6 0.2 fusion.68
  110.8 0.7 collective-permute-done.14
  111.5 0.6 fusion.20
  112.2 0.2 multiply_reduce_fusion.2
  112.4 0.1 fusion.66
  112.5 0.3 fusion.61
  112.8 0.2 split.22
  113.0 0.2 split.20
  113.2 0.4 fusion.32
  113.7 1.9 %collective-permute-start.16 = (f32[4,1,64,128]{3,2,1,0:T(8,128)S(1)}, f32[4,1,64,128]{3,2,1,0:T(8,128)S(1)}, u32[]{:S(2)}, u32[]{:S(2)}) collective-permute-start(f32[4,1,64,128]{3,2,1,0:T(8,128)S(1)} %pad_add_fusion.4), channel_id=1, source_target_pairs={{0,1},{1,2},{2,3},{3,4},{4,5},{5,6},{6,7},{7,8},{8,9},{9,10},{10,1... | collective-permute-start | bytes 393224 | tf_op jit(solution)/shard_map/ppermute | solution.py:20
  116.3 5.7 %collective-permute-done.16 = f32[4,1,64,128]{3,2,1,0:T(8,128)S(1)} collective-permute-done((f32[4,1,64,128]{3,2,1,0:T(8,128)S(1)}, f32[4,1,64,128]{3,2,1,0:T(8,128)S(1)}, u32[]{:S(2)}, u32[]{:S(2)}) %collective-permute-start.16) | collective-permute-done | bytes 131104 | tf_op jit(solution)/shard_map/ppermute | solution.py:20
  122.0 7.7 %collective-permute-start.17 = (f32[4,1,64,128]{3,2,1,0:T(8,128)S(1)}, f32[4,1,64,128]{3,2,1,0:T(8,128)S(1)}, u32[]{:S(2)}, u32[]{:S(2)}) collective-permute-start(f32[4,1,64,128]{3,2,1,0:T(8,128)S(1)} %get-tuple-element.21), channel_id=1, source_target_pairs={{1,0},{2,1},{3,2},{4,3},{5,4},{6,5},{7,6},{8,7},{9,8},{10,9},{11,1... | collective-permute-start | bytes 393224 | tf_op jit(solution)/shard_map/ppermute | solution.py:22
  129.7 0.1 pad_add_fusion
  129.8 0.8 collective-permute-done.17
  130.7 1.2 fusion.26
  131.8 0.8 copy.8
  (24 shorter events, 0.4 us)
Async XLA Ops:
  0.6 11.8 %copy-start = (f32[1,4,4,64,128]{4,3,2,1,0:T(8,128)S(1)}, f32[1,4,4,64,128]{4,3,2,1,0:T(8,128)}, u32[]{:S(2)}) copy-start(f32[1,4,4,64,128]{4,3,2,1,0:T(8,128)} %param.5) | copy-start | bytes 1572868
  1.7 11.3 %collective-permute-start.1 = (f32[4,1,64,128]{3,2,1,0:T(8,128)S(1)}, f32[4,1,64,128]{3,2,1,0:T(8,128)S(1)}, u32[]{:S(2)}, u32[]{:S(2)}) collective-permute-start(f32[4,1,64,128]{3,2,1,0:T(8,128)S(1)} %get-tuple-element.85), channel_id=1, source_target_pairs={{0,1},{1,2},{2,3},{3,4},{4,5},{5,6},{6,7},{7,8},{8,9},{9,10},{10,1... | collective-permute-start | bytes 393224 | tf_op jit(solution)/shard_map/ppermute | solution.py:20
  7.1 6.3 %collective-permute-start = (f32[4,1,64,128]{3,2,1,0:T(8,128)S(1)}, f32[4,1,64,128]{3,2,1,0:T(8,128)S(1)}, u32[]{:S(2)}, u32[]{:S(2)}) collective-permute-start(f32[4,1,64,128]{3,2,1,0:T(8,128)S(1)} %get-tuple-element.84), channel_id=1, source_target_pairs={{1,0},{2,1},{3,2},{4,3},{5,4},{6,5},{7,6},{8,7},{9,8},{10,9},{11,1... | collective-permute-start | bytes 393224 | tf_op jit(solution)/shard_map/ppermute | solution.py:22
  14.4 9.6 %collective-permute-start.3 = (f32[4,1,64,128]{3,2,1,0:T(8,128)S(1)}, f32[4,1,64,128]{3,2,1,0:T(8,128)S(1)}, u32[]{:S(2)}, u32[]{:S(2)}) collective-permute-start(f32[4,1,64,128]{3,2,1,0:T(8,128)S(1)} %get-tuple-element.76), channel_id=1, source_target_pairs={{0,1},{1,2},{2,3},{3,4},{4,5},{5,6},{6,7},{7,8},{8,9},{9,10},{10,1... | collective-permute-start | bytes 393224 | tf_op jit(solution)/shard_map/ppermute | solution.py:20
  16.4 8.4 %collective-permute-start.2 = (f32[4,1,64,128]{3,2,1,0:T(8,128)S(1)}, f32[4,1,64,128]{3,2,1,0:T(8,128)S(1)}, u32[]{:S(2)}, u32[]{:S(2)}) collective-permute-start(f32[4,1,64,128]{3,2,1,0:T(8,128)S(1)} %get-tuple-element.75), channel_id=1, source_target_pairs={{1,0},{2,1},{3,2},{4,3},{5,4},{6,5},{7,6},{8,7},{9,8},{10,9},{11,1... | collective-permute-start | bytes 393224 | tf_op jit(solution)/shard_map/ppermute | solution.py:22
  25.6 9.6 %collective-permute-start.5 = (f32[4,1,64,128]{3,2,1,0:T(8,128)S(1)}, f32[4,1,64,128]{3,2,1,0:T(8,128)S(1)}, u32[]{:S(2)}, u32[]{:S(2)}) collective-permute-start(f32[4,1,64,128]{3,2,1,0:T(8,128)S(1)} %get-tuple-element.70), channel_id=1, source_target_pairs={{0,1},{1,2},{2,3},{3,4},{4,5},{5,6},{6,7},{7,8},{8,9},{9,10},{10,1... | collective-permute-start | bytes 393224 | tf_op jit(solution)/shard_map/ppermute | solution.py:20
  27.5 8.4 %collective-permute-start.4 = (f32[4,1,64,128]{3,2,1,0:T(8,128)S(1)}, f32[4,1,64,128]{3,2,1,0:T(8,128)S(1)}, u32[]{:S(2)}, u32[]{:S(2)}) collective-permute-start(f32[4,1,64,128]{3,2,1,0:T(8,128)S(1)} %get-tuple-element.69), channel_id=1, source_target_pairs={{1,0},{2,1},{3,2},{4,3},{5,4},{6,5},{7,6},{8,7},{9,8},{10,9},{11,1... | collective-permute-start | bytes 393224 | tf_op jit(solution)/shard_map/ppermute | solution.py:22
  36.6 9.6 %collective-permute-start.7 = (f32[4,1,64,128]{3,2,1,0:T(8,128)S(1)}, f32[4,1,64,128]{3,2,1,0:T(8,128)S(1)}, u32[]{:S(2)}, u32[]{:S(2)}) collective-permute-start(f32[4,1,64,128]{3,2,1,0:T(8,128)S(1)} %get-tuple-element.64), channel_id=1, source_target_pairs={{0,1},{1,2},{2,3},{3,4},{4,5},{5,6},{6,7},{7,8},{8,9},{9,10},{10,1... | collective-permute-start | bytes 393224 | tf_op jit(solution)/shard_map/ppermute | solution.py:20
  38.6 8.4 %collective-permute-start.6 = (f32[4,1,64,128]{3,2,1,0:T(8,128)S(1)}, f32[4,1,64,128]{3,2,1,0:T(8,128)S(1)}, u32[]{:S(2)}, u32[]{:S(2)}) collective-permute-start(f32[4,1,64,128]{3,2,1,0:T(8,128)S(1)} %get-tuple-element.63), channel_id=1, source_target_pairs={{1,0},{2,1},{3,2},{4,3},{5,4},{6,5},{7,6},{8,7},{9,8},{10,9},{11,1... | collective-permute-start | bytes 393224 | tf_op jit(solution)/shard_map/ppermute | solution.py:22
  47.5 13.8 %collective-permute-start.8 = (f32[4,4,64,128]{3,2,1,0:T(8,128)S(1)}, f32[4,4,64,128]{3,2,1,0:T(8,128)S(1)}, u32[]{:S(2)}, u32[]{:S(2)}) collective-permute-start(f32[4,4,64,128]{3,2,1,0:T(8,128)S(1)} %fusion.12), channel_id=1, source_target_pairs={{480,0},{0,32},{32,64},{64,96},{96,128},{128,160},{160,192},{192,2... | collective-permute-start | bytes 1572872 | tf_op jit(solution)/shard_map/ppermute | solution.py:32
  61.6 11.4 %collective-permute-start.9 = (f32[4,4,64,128]{3,2,1,0:T(8,128)S(1)}, f32[4,4,64,128]{3,2,1,0:T(8,128)S(1)}, u32[]{:S(2)}, u32[]{:S(2)}) collective-permute-start(f32[4,4,64,128]{3,2,1,0:T(8,128)S(1)} %fusion.29), channel_id=1, source_target_pairs={{32,0},{64,32},{96,64},{128,96},{160,128},{192,160},{224,192},{256... | collective-permute-start | bytes 1572872 | tf_op jit(solution)/shard_map/ppermute | solution.py:32
  73.1 12.3 %collective-permute-start.11 = (f32[4,1,64,128]{3,2,1,0:T(8,128)S(1)}, f32[4,1,64,128]{3,2,1,0:T(8,128)S(1)}, u32[]{:S(2)}, u32[]{:S(2)}) collective-permute-start(f32[4,1,64,128]{3,2,1,0:T(8,128)S(1)} %get-tuple-element.54), channel_id=1, source_target_pairs={{0,1},{1,2},{2,3},{3,4},{4,5},{5,6},{6,7},{7,8},{8,9},{9,10},{10,1... | collective-permute-start | bytes 393224 | tf_op jit(solution)/shard_map/ppermute | solution.py:20
  83.0 6.3 %collective-permute-start.10 = (f32[4,1,64,128]{3,2,1,0:T(8,128)S(1)}, f32[4,1,64,128]{3,2,1,0:T(8,128)S(1)}, u32[]{:S(2)}, u32[]{:S(2)}) collective-permute-start(f32[4,1,64,128]{3,2,1,0:T(8,128)S(1)} %get-tuple-element.53), channel_id=1, source_target_pairs={{1,0},{2,1},{3,2},{4,3},{5,4},{6,5},{7,6},{8,7},{9,8},{10,9},{11,1... | collective-permute-start | bytes 393224 | tf_op jit(solution)/shard_map/ppermute | solution.py:22
  90.0 9.7 %collective-permute-start.13 = (f32[4,1,64,128]{3,2,1,0:T(8,128)S(1)}, f32[4,1,64,128]{3,2,1,0:T(8,128)S(1)}, u32[]{:S(2)}, u32[]{:S(2)}) collective-permute-start(f32[4,1,64,128]{3,2,1,0:T(8,128)S(1)} %get-tuple-element.48), channel_id=1, source_target_pairs={{0,1},{1,2},{2,3},{3,4},{4,5},{5,6},{6,7},{7,8},{8,9},{9,10},{10,1... | collective-permute-start | bytes 393224 | tf_op jit(solution)/shard_map/ppermute | solution.py:20
  92.0 8.5 %collective-permute-start.12 = (f32[4,1,64,128]{3,2,1,0:T(8,128)S(1)}, f32[4,1,64,128]{3,2,1,0:T(8,128)S(1)}, u32[]{:S(2)}, u32[]{:S(2)}) collective-permute-start(f32[4,1,64,128]{3,2,1,0:T(8,128)S(1)} %get-tuple-element.47), channel_id=1, source_target_pairs={{1,0},{2,1},{3,2},{4,3},{5,4},{6,5},{7,6},{8,7},{9,8},{10,9},{11,1... | collective-permute-start | bytes 393224 | tf_op jit(solution)/shard_map/ppermute | solution.py:22
  101.2 9.6 %collective-permute-start.15 = (f32[4,1,64,128]{3,2,1,0:T(8,128)S(1)}, f32[4,1,64,128]{3,2,1,0:T(8,128)S(1)}, u32[]{:S(2)}, u32[]{:S(2)}) collective-permute-start(f32[4,1,64,128]{3,2,1,0:T(8,128)S(1)} %get-tuple-element.46), channel_id=1, source_target_pairs={{0,1},{1,2},{2,3},{3,4},{4,5},{5,6},{6,7},{7,8},{8,9},{9,10},{10,1... | collective-permute-start | bytes 393224 | tf_op jit(solution)/shard_map/ppermute | solution.py:20
  103.1 8.4 %collective-permute-start.14 = (f32[4,1,64,128]{3,2,1,0:T(8,128)S(1)}, f32[4,1,64,128]{3,2,1,0:T(8,128)S(1)}, u32[]{:S(2)}, u32[]{:S(2)}) collective-permute-start(f32[4,1,64,128]{3,2,1,0:T(8,128)S(1)} %get-tuple-element.45), channel_id=1, source_target_pairs={{1,0},{2,1},{3,2},{4,3},{5,4},{6,5},{7,6},{8,7},{9,8},{10,9},{11,1... | collective-permute-start | bytes 393224 | tf_op jit(solution)/shard_map/ppermute | solution.py:22
  113.7 8.3 %collective-permute-start.16 = (f32[4,1,64,128]{3,2,1,0:T(8,128)S(1)}, f32[4,1,64,128]{3,2,1,0:T(8,128)S(1)}, u32[]{:S(2)}, u32[]{:S(2)}) collective-permute-start(f32[4,1,64,128]{3,2,1,0:T(8,128)S(1)} %pad_add_fusion.4), channel_id=1, source_target_pairs={{0,1},{1,2},{2,3},{3,4},{4,5},{5,6},{6,7},{7,8},{8,9},{9,10},{10,1... | collective-permute-start | bytes 393224 | tf_op jit(solution)/shard_map/ppermute | solution.py:20
  122.0 8.7 %collective-permute-start.17 = (f32[4,1,64,128]{3,2,1,0:T(8,128)S(1)}, f32[4,1,64,128]{3,2,1,0:T(8,128)S(1)}, u32[]{:S(2)}, u32[]{:S(2)}) collective-permute-start(f32[4,1,64,128]{3,2,1,0:T(8,128)S(1)} %get-tuple-element.21), channel_id=1, source_target_pairs={{1,0},{2,1},{3,2},{4,3},{5,4},{6,5},{7,6},{8,7},{9,8},{10,9},{11,1... | collective-permute-start | bytes 393224 | tf_op jit(solution)/shard_map/ppermute | solution.py:22
where the time goes:
time: 133 us
  starting transfers between devices  88.3 us (66%)
  waiting for transfers between devices  29.9 us (22%)
  other arithmetic  6.76 us (5%)
  local copies, waits for them, and re-layouts  5.34 us (4%)
  between operations  2.37 us (2%)
    ppermute x8, starting transfers between devices, with_halo(): lax.ppermute(head, axis, [((i + 1) % count, i) for i in range(count)])  52.2 us
    ppermute x8, starting transfers between devices, with_halo(): lax.ppermute(tail, axis, [(i, (i + 1) % count) for i in range(count)])  26.8 us
    ppermute x2, waiting for transfers between devices, shifted(): return lax.ppermute(block, axis, route)  15.3 us
    ppermute x2, starting transfers between devices, shifted(): return lax.ppermute(block, axis, route)  9.22 us
    ppermute x8, waiting for transfers between devices, with_halo(): lax.ppermute(head, axis, [((i + 1) % count, i) for i in range(count)])  8.89 us
    ppermute x8, waiting for transfers between devices, with_halo(): lax.ppermute(tail, axis, [(i, (i + 1) % count) for i in range(count)])  5.68 us
  transfers between devices with their start and end apart: 18, of which 11 were waited for; matrix products, arithmetic and copies ran while one was open for 2% of the time, Pallas kernels for 0%

commit v1 on v0

v1 whole, which is shorter than its diff:
```python
import jax
import jax.numpy as jnp
from jax import lax
from jax.experimental import pallas as pl
from jax.experimental.pallas import tpu as pltpu
from jax.sharding import PartitionSpec as P

SWEEPS = 3
TAU = 0.2
HALF_TAU = 0.5 * TAU
VISCOUS = 1.0
SCALE = 1.0 / (1.0 + 6.0 * VISCOUS)


def base_speed(shape):
    rows = shape[0]
    cell = lax.broadcasted_iota(jnp.int32, shape, 0).astype(jnp.float32)
    radius = 1.0 + (cell + 0.5) / rows
    return 0.2 + 0.6 / (radius * radius)


def lane_up(f):
    return pltpu.roll(f, f.shape[1] - 1, 1)


def lane_down(f):
    return pltpu.roll(f, 1, 1)


class Walls:
    def __init__(self, shape):
        row = lax.broadcasted_iota(jnp.int32, shape, 0)
        self.first = row == 0
        self.last = row == shape[0] - 1
        self.rows = shape[0]

    def up(self, f):
        return jnp.where(self.last, 0.0, pltpu.roll(f, self.rows - 1, 0))

    def down(self, f):
        return jnp.where(self.first, 0.0, pltpu.roll(f, 1, 0))


def place(layer, depth, odd):
    k = layer % depth
    return k + odd * (depth - 1 - 2 * k)


def layer_of(refs, field, layer, depth, odd):
    behind, own, ahead = refs
    ref = behind if layer < 0 else own if layer < depth else ahead
    return ref[field, place(layer, depth, odd)]


def in_plane(f, walls):
    return lane_up(f) + lane_down(f) + walls.up(f) + walls.down(f)


def forward_kernel(own, chip, cross, ends, force, first, second):
    fields, depth, rows, columns = own.shape
    odd = lax.axis_index("gz") % 2
    sign = (1 - 2 * odd).astype(jnp.float32)
    walls = Walls((rows, columns))
    speed = base_speed((rows, columns))
    refs = (cross, own, chip)

    def at(field, layer):
        return layer_of(refs, field, layer, depth, odd)

    reach = SWEEPS
    for layer in range(-reach, depth + reach):
        here = [at(f, layer) for f in range(fields)]
        d_z = [at(f, layer + 1) - at(f, layer - 1) for f in range(fields)]
        d_th = [lane_up(f) - lane_down(f) for f in here]
        d_r = [walls.up(f) - walls.down(f) for f in here]
        u, v, w, p = here
        by_th = HALF_TAU * (speed + v)
        by_r = HALF_TAU * u
        by_z = (HALF_TAU * sign) * w
        to = layer + reach
        carried = [by_th * d_th[f] + by_r * d_r[f] + by_z * d_z[f] for f in range(3)]
        force[0, to] = u - (carried[0] + HALF_TAU * d_r[3]) + (2.0 * TAU) * speed * v
        force[1, to] = v - (carried[1] + HALF_TAU * d_th[3]) - TAU * speed * u
        force[2, to] = w - (carried[2] + (HALF_TAU * sign) * d_z[3])
        force[3, to] = p - HALF_TAU * (d_r[0] + d_th[1] + sign * d_z[2])

    def sweep(source, source_reach, put):
        reach = source_reach - 1
        for layer in range(-reach, depth + reach):
            for f in range(fields):
                k = layer + source_reach
                total = force[f, layer + SWEEPS] + source[f, k - 1] + source[f, k + 1]
                total = total + in_plane(source[f, k], walls)
                put(f, layer, total * SCALE)

    def put_first(f, layer, value):
        first[f, layer + 2] = value

    def put_second(f, layer, value):
        second[f, layer + 1] = value

    def put_ends(f, layer, value):
        ends[f, place(layer, depth, odd)] = value

    sweep(force, 3, put_first)
    sweep(first, 2, put_second)
    sweep(second, 1, put_ends)


def turn(field, amount):
    return pltpu.roll(field, amount, 1)


def mismatch_kernel(shift, ends, following, mismatch):
    fields, depth, rows, columns = ends.shape
    last = lax.axis_index("tm") == lax.axis_size("tm") - 1
    amount = jnp.where(last, shift[0], 0)
    for f in range(fields):
        for k in range(depth):
            mismatch[f, k] = ends[f, k] - turn(following[f, k], amount)


def adjoint_kernel(
    shift, step_size, own, chip, cross, own_mis, chip_mis, cross_mis, prior_ends, updated, cot, first, second
):
    fields, depth, rows, columns = own.shape
    odd = lax.axis_index("gz") % 2
    sign = (1 - 2 * odd).astype(jnp.float32)
    walls = Walls((rows, columns))
    speed = base_speed((rows, columns))
    refs = (cross, own, chip)
    mis = (cross_mis, own_mis, chip_mis)

    def at(field, layer):
        return layer_of(refs, field, layer, depth, odd)

    def mis_at(field, layer):
        return layer_of(mis, field, layer, depth, odd)

    for f in range(fields):
        for layer in range(-3, depth + 3):
            here = mis_at(f, layer)
            total = mis_at(f, layer - 1) + mis_at(f, layer + 1) + in_plane(here, walls)
            total = total * SCALE
            first[f, layer + 3] = total
            if -1 <= layer <= depth:
                cot[f, layer + 1] = (here + total) * SCALE
        for layer in range(-2, depth + 2):
            k = layer + 3
            total = first[f, k - 1] + first[f, k + 1] + in_plane(first[f, k], walls)
            total = total * SCALE
            second[f, layer + 2] = total
            if -1 <= layer <= depth:
                cot[f, layer + 1] = cot[f, layer + 1] + total * SCALE
        for layer in range(-1, depth + 1):
            k = layer + 2
            total = second[f, k - 1] + second[f, k + 1] + in_plane(second[f, k], walls)
            cot[f, layer + 1] = cot[f, layer + 1] + total * SCALE

    is_first = lax.axis_index("tm") == 0
    amount = jnp.where(is_first, columns - shift[0], 0) % columns
    size = step_size[0]
    half = HALF_TAU
    for layer in range(depth):
        k = layer + 1
        here = [at(f, layer) for f in range(fields)]
        u, v, w, p = here
        c = [cot[f, k] for f in range(fields)]
        below = [cot[f, k - 1] for f in range(fields)]
        above = [cot[f, k + 1] for f in range(fields)]
        w_below, w_above = at(2, layer - 1), at(2, layer + 1)
        d_z = [at(f, layer + 1) - at(f, layer - 1) for f in range(3)]
        d_th = [lane_up(f) - lane_down(f) for f in here[:3]]
        d_r = [walls.up(f) - walls.down(f) for f in here[:3]]
        swirl = speed + v

        def th(f):
            return lane_up(f) - lane_down(f)

        def rad(f):
            return walls.up(f) - walls.down(f)

        pull_r = c[0] * d_r[0] + c[1] * d_r[1] + c[2] * d_r[2]
        pull_th = c[0] * d_th[0] + c[1] * d_th[1] + c[2] * d_th[2]
        pull_z = c[0] * d_z[0] + c[1] * d_z[1] + c[2] * d_z[2]
        axial = [w_above * above[f] - w_below * below[f] for f in range(3)]
        grads = [
            c[0]
            + half * (th(swirl * c[0]) + rad(u * c[0] + c[3]) + sign * axial[0] - pull_r)
            - TAU * speed * c[1],
            c[1]
            + half * (th(swirl * c[1] + c[3]) + rad(u * c[1]) + sign * axial[1] - pull_th)
            + (2.0 * TAU) * speed * c[0],
            c[2]
            + half
            * (
                th(swirl * c[2])
                + rad(u * c[2])
                + sign * (axial[2] + above[3] - below[3] - pull_z)
            ),
            c[3] + half * (rad(c[0]) + th(c[1]) + sign * (above[2] - below[2])),
        ]
        to = place(layer, depth, odd)
        for f in range(fields):
            prior = turn(prior_ends[f, to], amount) - here[f]
            updated[f, to] = here[f] - size * (grads[f] - prior)


VMEM = pl.BlockSpec(memory_space=pltpu.VMEM)
PARAMS = pltpu.CompilerParams(vmem_limit_bytes=16 * 2**20)
SMEM = pl.BlockSpec(memory_space=pltpu.SMEM)


def scratch(shape, layers):
    return pltpu.VMEM((shape[0], layers) + shape[2:], jnp.float32)


def cost(shape, passes):
    size = shape[0] * shape[1] * shape[2] * shape[3]
    return pl.CostEstimate(flops=passes * size, bytes_accessed=4 * size, transcendentals=0)


def forward(own, chip, cross):
    shape = own.shape
    depth = shape[1]
    return pl.pallas_call(
        forward_kernel,
        out_shape=jax.ShapeDtypeStruct(shape, jnp.float32),
        in_specs=[VMEM] * 3,
        out_specs=VMEM,
        scratch_shapes=[scratch(shape, depth + 6), scratch(shape, depth + 4), scratch(shape, depth + 2)],
        cost_estimate=cost(shape, 100),
        compiler_params=PARAMS,
        name="forward",
    )(own, chip, cross)


def compare(shift, ends, following):
    return pl.pallas_call(
        mismatch_kernel,
        out_shape=jax.ShapeDtypeStruct(ends.shape, jnp.float32),
        in_specs=[SMEM, VMEM, VMEM],
        out_specs=VMEM,
        cost_estimate=cost(ends.shape, 2),
        compiler_params=PARAMS,
        name="compare",
    )(shift, ends, following)


def adjoint(shift, step_size, slabs, mismatches, prior_ends):
    shape = prior_ends.shape
    depth = shape[1]
    return pl.pallas_call(
        adjoint_kernel,
        out_shape=jax.ShapeDtypeStruct(shape, jnp.float32),
        in_specs=[SMEM, SMEM] + [VMEM] * 7,
        out_specs=VMEM,
        scratch_shapes=[scratch(shape, depth + 2), scratch(shape, depth + 6), scratch(shape, depth + 4)],
        cost_estimate=cost(shape, 150),
        compiler_params=PARAMS,
        name="adjoint",
    )(shift, step_size, *slabs, *mismatches, prior_ends)


def per_device(states, shift, step_size):
    start = states[0]
    slabs, sections = lax.axis_size("gz"), lax.axis_size("tm")
    same_chip = [(i, i ^ 1) for i in range(slabs)]
    next_chip = [(i, (i + 1 if i % 2 else i - 1) % slabs) for i in range(slabs)]
    forth = [(i, (i + 1) % sections) for i in range(sections)]
    back = [((i + 1) % sections, i) for i in range(sections)]

    cross = lax.ppermute(start, "gz", next_chip)
    chip = lax.ppermute(start, "gz", same_chip)
    following = lax.ppermute(start, "tm", back)
    ends = forward(start, chip, cross)
    prior_ends = lax.ppermute(ends, "tm", forth)
    mismatch = compare(shift, ends, following)
    cross_mis = lax.ppermute(mismatch, "gz", next_chip)
    chip_mis = lax.ppermute(mismatch, "gz", same_chip)
    updated = adjoint(shift, step_size, (start, chip, cross), (mismatch, chip_mis, cross_mis), prior_ends)
    return updated[None], mismatch[None]


def solution(mesh):
    placed = P("tm", None, "gz", None, None)
    return jax.shard_map(
        per_device,
        mesh=mesh,
        in_specs=(placed, P(), P()),
        out_specs=(placed, placed),
        check_vma=False,
    )
```

time: 133 us -> 66.1 us (0.50)
  the two profiles are of different devices: /device:TPU:1 before, /device:TPU:2 now
where the time goes in v1:
time: 66.1 us; the launch traced here: 65.7 us
  starting transfers between devices  33.6 us (51%)
  waiting for transfers between devices  20.8 us (31%)
  Pallas kernels  7.19 us (11%)
  local copies, waits for them, and re-layouts  2.09 us (3%)
  between operations  2.01 us (3%)
    ppermute x1, waiting for transfers between devices, per_device(): prior_ends = lax.ppermute(ends, 'tm', forth)  11.9 us
    ppermute x1, starting transfers between devices, per_device(): cross = lax.ppermute(start, 'gz', next_chip)  11 us
    ppermute x1, starting transfers between devices, per_device(): cross_mis = lax.ppermute(mismatch, 'gz', next_chip)  7.95 us
    ppermute x1, starting transfers between devices, per_device(): following = lax.ppermute(start, 'tm', back)  7.23 us
    pallas_call x1, Pallas kernels, adjoint(): pl.pallas_call(adjoint_kernel, out_shape=jax.ShapeDtypeStruct(shape, jnp....  3.63 us
    ppermute x1, starting transfers between devices, per_device(): prior_ends = lax.ppermute(ends, 'tm', forth)  3.55 us
    ppermute x1, waiting for transfers between devices, per_device(): cross = lax.ppermute(start, 'gz', next_chip)  3.11 us
    ppermute x1, waiting for transfers between devices, per_device(): cross_mis = lax.ppermute(mismatch, 'gz', next_chip)  2.95 us
  transfers between devices with their start and end apart: 6, of which 4 were waited for; matrix products, arithmetic and copies ran while one was open for 0% of the time, Pallas kernels for 4%

profile of v1, /device:TPU:2, one launch (start us, length us, event | category | flops | bytes accessed | tf_op | source)
XLA Modules:
  0.0 65.7 jit_solution(15342019689358529984)
XLA Ops:
  0.6 1.9 %collective-permute-start = (f32[4,4,64,128]{3,2,1,0:T(8,128)}, f32[4,4,64,128]{3,2,1,0:T(8,128)S(1)}, u32[]{:S(2)}, u32[]{:S(2)}) collective-permute-start(f32[4,4,64,128]{3,2,1,0:T(8,128)} %bitcast.4), channel_id=1, source_target_pairs={{0,1},{1,0},{2,3},{3,2},{4,5},{5,4},{6,7},{7,6},{8,9},{9,8},{10,11... | collective-permute-start | bytes 1572872 | tf_op jit(solution)/shard_map/ppermute | solution.py:274
  2.6 11.0 %collective-permute-start.1 = (f32[4,4,64,128]{3,2,1,0:T(8,128)}, f32[4,4,64,128]{3,2,1,0:T(8,128)S(1)}, u32[]{:S(2)}, u32[]{:S(2)}) collective-permute-start(f32[4,4,64,128]{3,2,1,0:T(8,128)} %bitcast.5), channel_id=1, source_target_pairs={{0,31},{1,2},{2,1},{3,4},{4,3},{5,6},{6,5},{7,8},{8,7},{9,10},{10,... | collective-permute-start | bytes 1572872 | tf_op jit(solution)/shard_map/ppermute | solution.py:273
  13.6 7.2 %collective-permute-start.2 = (f32[4,4,64,128]{3,2,1,0:T(8,128)}, f32[4,4,64,128]{3,2,1,0:T(8,128)S(1)}, u32[]{:S(2)}, u32[]{:S(2)}) collective-permute-start(f32[4,4,64,128]{3,2,1,0:T(8,128)} %bitcast.6), channel_id=1, source_target_pairs={{32,0},{64,32},{96,64},{128,96},{160,128},{192,160},{224,192},{256... | collective-permute-start | bytes 1572872 | tf_op jit(solution)/shard_map/ppermute | solution.py:275
  21.5 0.0 collective-permute-done.chip
  21.5 3.1 %collective-permute-done.1.cross = f32[4,4,64,128]{3,2,1,0:T(8,128)S(1)} collective-permute-done((f32[4,4,64,128]{3,2,1,0:T(8,128)}, f32[4,4,64,128]{3,2,1,0:T(8,128)S(1)}, u32[]{:S(2)}, u32[]{:S(2)}) %collective-permute-start.1) | collective-permute-done | bytes 524320 | tf_op jit(solution)/shard_map/ppermute | solution.py:273
  24.6 0.0 copy-start.1
  24.6 1.0 %copy-done.1 = f32[1,4,4,64,128]{4,3,2,1,0:T(8,128)S(1)} copy-done((f32[1,4,4,64,128]{4,3,2,1,0:T(8,128)S(1)}, f32[1,4,4,64,128]{4,3,2,1,0:T(8,128)}, u32[]{:S(2)}) %copy-start.1) | copy-done | bytes 524312
  25.6 2.6 %forward.1.ends = f32[4,4,64,128]{3,2,1,0:T(8,128)S(1)} custom-call(f32[4,4,64,128]{3,2,1,0:T(8,128)S(1)} %bitcast.7, f32[4,4,64,128]{3,2,1,0:T(8,128)S(1)} %collective-permute-done.chip, f32[4,4,64,128]{3,2,1,0:T(8,128)S(1)} %collective-permute-done.1.cross), custom_call_target="tpu_custom_call" | custom-call | flops 13107200 | bytes 524288 | tf_op jit(solution)/shard_map/forward/pallas_call | solution.py:226
  28.2 0.0 copy-start.2
  28.2 2.9 %collective-permute-done.2.following = f32[4,4,64,128]{3,2,1,0:T(8,128)S(1)} collective-permute-done((f32[4,4,64,128]{3,2,1,0:T(8,128)}, f32[4,4,64,128]{3,2,1,0:T(8,128)S(1)}, u32[]{:S(2)}, u32[]{:S(2)}) %collective-permute-start.2) | collective-permute-done | bytes 524320 | tf_op jit(solution)/shard_map/ppermute | solution.py:275
  31.1 1.0 %compare.1.own_mis = f32[4,4,64,128]{3,2,1,0:T(8,128)} custom-call(s32[1]{0:T(128)S(6)} %copy.5.shift, f32[4,4,64,128]{3,2,1,0:T(8,128)S(1)} %forward.1.ends, f32[4,4,64,128]{3,2,1,0:T(8,128)S(1)} %collective-permute-done.2.following), custom_call_target="tpu_custom_call" | custom-call | flops 262144 | bytes 524288 | tf_op jit(solution)/shard_map/compare/pallas_call | solution.py:239
  32.1 1.9 %collective-permute-start.3 = (f32[4,4,64,128]{3,2,1,0:T(8,128)}, f32[4,4,64,128]{3,2,1,0:T(8,128)S(1)}, u32[]{:S(2)}, u32[]{:S(2)}) collective-permute-start(f32[4,4,64,128]{3,2,1,0:T(8,128)} %compare.1.own_mis), channel_id=1, source_target_pairs={{0,1},{1,0},{2,3},{3,2},{4,5},{5,4},{6,7},{7,6},{8,9},{9,8},{10,11... | collective-permute-start | bytes 1572872 | tf_op jit(solution)/shard_map/ppermute | solution.py:280
  34.0 8.0 %collective-permute-start.4 = (f32[4,4,64,128]{3,2,1,0:T(8,128)}, f32[4,4,64,128]{3,2,1,0:T(8,128)S(1)}, u32[]{:S(2)}, u32[]{:S(2)}) collective-permute-start(f32[4,4,64,128]{3,2,1,0:T(8,128)} %compare.1.own_mis), channel_id=1, source_target_pairs={{0,31},{1,2},{2,1},{3,4},{4,3},{5,6},{6,5},{7,8},{8,7},{9,10},{10,... | collective-permute-start | bytes 1572872 | tf_op jit(solution)/shard_map/ppermute | solution.py:279
  42.0 3.5 %collective-permute-start.5 = (f32[4,4,64,128]{3,2,1,0:T(8,128)S(1)}, f32[4,4,64,128]{3,2,1,0:T(8,128)S(1)}, u32[]{:S(2)}, u32[]{:S(2)}) collective-permute-start(f32[4,4,64,128]{3,2,1,0:T(8,128)S(1)} %forward.1.ends), channel_id=1, source_target_pairs={{0,32},{32,64},{64,96},{96,128},{128,160},{160,192},{192,224},{224... | collective-permute-start | bytes 1572872 | tf_op jit(solution)/shard_map/ppermute | solution.py:277
  46.2 0.0 collective-permute-done.3.chip_mis
  46.2 2.9 %collective-permute-done.4.cross_mis = f32[4,4,64,128]{3,2,1,0:T(8,128)S(1)} collective-permute-done((f32[4,4,64,128]{3,2,1,0:T(8,128)}, f32[4,4,64,128]{3,2,1,0:T(8,128)S(1)}, u32[]{:S(2)}, u32[]{:S(2)}) %collective-permute-start.4) | collective-permute-done | bytes 524320 | tf_op jit(solution)/shard_map/ppermute | solution.py:279
  49.1 11.9 %collective-permute-done.5.prior_ends = f32[4,4,64,128]{3,2,1,0:T(8,128)S(1)} collective-permute-done((f32[4,4,64,128]{3,2,1,0:T(8,128)S(1)}, f32[4,4,64,128]{3,2,1,0:T(8,128)S(1)}, u32[]{:S(2)}, u32[]{:S(2)}) %collective-permute-start.5) | collective-permute-done | bytes 524320 | tf_op jit(solution)/shard_map/ppermute | solution.py:277
  61.0 0.0 copy-done.2
  61.0 0.0 copy-start
  61.0 1.0 %copy-done = f32[4,4,64,128]{3,2,1,0:T(8,128)S(1)} copy-done((f32[4,4,64,128]{3,2,1,0:T(8,128)S(1)}, f32[4,4,64,128]{3,2,1,0:T(8,128)}, u32[]{:S(2)}) %copy-start) | copy-done | bytes 524312
  62.1 3.6 %adjoint.1 = f32[4,4,64,128]{3,2,1,0:T(8,128)} custom-call(s32[1]{0:T(128)S(6)} %copy.5.shift, f32[1]{0:T(128)S(6)} %copy.6.step_size, f32[4,4,64,128]{3,2,1,0:T(8,128)S(1)} %bitcast.8, f32[4,4,64,128]{3,2,1,0:T(8,128)S(1)} %collective-permute-done.chip, f32[4,4,64,128]{3,2,1,0:T(8,128)S(1)} %collective-permute-done.1.cross, f32[4,4,64,128]{3,2,1,0:T(8,128)S(1)} %copy-done, ...), custom_call_target="tpu_custom_call" | custom-call | flops 19660800 | bytes 524288 | tf_op jit(solution)/shard_map/adjoint/pallas_call | solution.py:253
Async XLA Ops:
  0.6 20.9 %collective-permute-start = (f32[4,4,64,128]{3,2,1,0:T(8,128)}, f32[4,4,64,128]{3,2,1,0:T(8,128)S(1)}, u32[]{:S(2)}, u32[]{:S(2)}) collective-permute-start(f32[4,4,64,128]{3,2,1,0:T(8,128)} %bitcast.4), channel_id=1, source_target_pairs={{0,1},{1,0},{2,3},{3,2},{4,5},{5,4},{6,7},{7,6},{8,9},{9,8},{10,11... | collective-permute-start | bytes 1572872 | tf_op jit(solution)/shard_map/ppermute | solution.py:274
  2.6 22.0 %collective-permute-start.1 = (f32[4,4,64,128]{3,2,1,0:T(8,128)}, f32[4,4,64,128]{3,2,1,0:T(8,128)S(1)}, u32[]{:S(2)}, u32[]{:S(2)}) collective-permute-start(f32[4,4,64,128]{3,2,1,0:T(8,128)} %bitcast.5), channel_id=1, source_target_pairs={{0,31},{1,2},{2,1},{3,4},{4,3},{5,6},{6,5},{7,8},{8,7},{9,10},{10,... | collective-permute-start | bytes 1572872 | tf_op jit(solution)/shard_map/ppermute | solution.py:273
  13.6 17.5 %collective-permute-start.2 = (f32[4,4,64,128]{3,2,1,0:T(8,128)}, f32[4,4,64,128]{3,2,1,0:T(8,128)S(1)}, u32[]{:S(2)}, u32[]{:S(2)}) collective-permute-start(f32[4,4,64,128]{3,2,1,0:T(8,128)} %bitcast.6), channel_id=1, source_target_pairs={{32,0},{64,32},{96,64},{128,96},{160,128},{192,160},{224,192},{256... | collective-permute-start | bytes 1572872 | tf_op jit(solution)/shard_map/ppermute | solution.py:275
  24.6 1.0 %copy-start.1 = (f32[1,4,4,64,128]{4,3,2,1,0:T(8,128)S(1)}, f32[1,4,4,64,128]{4,3,2,1,0:T(8,128)}, u32[]{:S(2)}) copy-start(f32[1,4,4,64,128]{4,3,2,1,0:T(8,128)} %param.3) | copy-start | bytes 1572868
  28.2 32.8 %copy-start.2 = (f32[1,4,4,64,128]{4,3,2,1,0:T(8,128)S(1)}, f32[1,4,4,64,128]{4,3,2,1,0:T(8,128)}, u32[]{:S(2)}) copy-start(f32[1,4,4,64,128]{4,3,2,1,0:T(8,128)} %param.3) | copy-start | bytes 1572868
  32.1 14.1 %collective-permute-start.3 = (f32[4,4,64,128]{3,2,1,0:T(8,128)}, f32[4,4,64,128]{3,2,1,0:T(8,128)S(1)}, u32[]{:S(2)}, u32[]{:S(2)}) collective-permute-start(f32[4,4,64,128]{3,2,1,0:T(8,128)} %compare.1.own_mis), channel_id=1, source_target_pairs={{0,1},{1,0},{2,3},{3,2},{4,5},{5,4},{6,7},{7,6},{8,9},{9,8},{10,11... | collective-permute-start | bytes 1572872 | tf_op jit(solution)/shard_map/ppermute | solution.py:280
  34.0 15.1 %collective-permute-start.4 = (f32[4,4,64,128]{3,2,1,0:T(8,128)}, f32[4,4,64,128]{3,2,1,0:T(8,128)S(1)}, u32[]{:S(2)}, u32[]{:S(2)}) collective-permute-start(f32[4,4,64,128]{3,2,1,0:T(8,128)} %compare.1.own_mis), channel_id=1, source_target_pairs={{0,31},{1,2},{2,1},{3,4},{4,3},{5,6},{6,5},{7,8},{8,7},{9,10},{10,... | collective-permute-start | bytes 1572872 | tf_op jit(solution)/shard_map/ppermute | solution.py:279
  42.0 19.1 %collective-permute-start.5 = (f32[4,4,64,128]{3,2,1,0:T(8,128)S(1)}, f32[4,4,64,128]{3,2,1,0:T(8,128)S(1)}, u32[]{:S(2)}, u32[]{:S(2)}) collective-permute-start(f32[4,4,64,128]{3,2,1,0:T(8,128)S(1)} %forward.1.ends), channel_id=1, source_target_pairs={{0,32},{32,64},{64,96},{96,128},{128,160},{160,192},{192,224},{224... | collective-permute-start | bytes 1572872 | tf_op jit(solution)/shard_map/ppermute | solution.py:277
  61.0 1.0 %copy-start = (f32[4,4,64,128]{3,2,1,0:T(8,128)S(1)}, f32[4,4,64,128]{3,2,1,0:T(8,128)}, u32[]{:S(2)}) copy-start(f32[4,4,64,128]{3,2,1,0:T(8,128)} %compare.1.own_mis) | copy-start | bytes 1572868

commit v2 on v1

v2 whole, which is shorter than its diff:
```python
import jax
import jax.numpy as jnp
from jax import lax
from jax.experimental import pallas as pl
from jax.experimental.pallas import tpu as pltpu
from jax.sharding import PartitionSpec as P

SWEEPS = 3
TAU = 0.2
HALF_TAU = 0.5 * TAU
VISCOUS = 1.0
SCALE = 1.0 / (1.0 + 6.0 * VISCOUS)


def base_speed(shape):
    rows = shape[0]
    cell = lax.broadcasted_iota(jnp.int32, shape, 0).astype(jnp.float32)
    radius = 1.0 + (cell + 0.5) / rows
    return 0.2 + 0.6 / (radius * radius)


def lane_up(f):
    return pltpu.roll(f, f.shape[1] - 1, 1)


def lane_down(f):
    return pltpu.roll(f, 1, 1)


class Walls:
    def __init__(self, shape):
        row = lax.broadcasted_iota(jnp.int32, shape, 0)
        self.first = row == 0
        self.last = row == shape[0] - 1
        self.rows = shape[0]

    def up(self, f):
        return jnp.where(self.last, 0.0, pltpu.roll(f, self.rows - 1, 0))

    def down(self, f):
        return jnp.where(self.first, 0.0, pltpu.roll(f, 1, 0))


def place(layer, depth, odd):
    k = layer % depth
    return k + odd * (depth - 1 - 2 * k)


def layer_of(refs, field, layer, depth, odd):
    behind, own, ahead = refs
    ref = behind if layer < 0 else own if layer < depth else ahead
    return ref[field, place(layer, depth, odd)]


def in_plane(f, walls):
    return lane_up(f) + lane_down(f) + walls.up(f) + walls.down(f)


def explicit(at, put, layers, sign, walls, speed):
    for layer in layers:
        here = [at(f, layer) for f in range(4)]
        d_z = [at(f, layer + 1) - at(f, layer - 1) for f in range(4)]
        d_th = [lane_up(f) - lane_down(f) for f in here]
        d_r = [walls.up(f) - walls.down(f) for f in here]
        u, v, w, p = here
        by_th = HALF_TAU * (speed + v)
        by_r = HALF_TAU * u
        by_z = (HALF_TAU * sign) * w
        carried = [by_th * d_th[f] + by_r * d_r[f] + by_z * d_z[f] for f in range(3)]
        put(0, layer, u - (carried[0] + HALF_TAU * d_r[3]) + (2.0 * TAU) * speed * v)
        put(1, layer, v - (carried[1] + HALF_TAU * d_th[3]) - TAU * speed * u)
        put(2, layer, w - (carried[2] + (HALF_TAU * sign) * d_z[3]))
        put(3, layer, p - HALF_TAU * (d_r[0] + d_th[1] + sign * d_z[2]))


def neighbours(at, field, layer, walls):
    return at(field, layer - 1) + at(field, layer + 1) + in_plane(at(field, layer), walls)


class Level:
    def __init__(self, *parts):
        self.parts = parts

    def find(self, layer):
        for ref, low, high, start in self.parts:
            if low <= layer < high:
                return ref, start + layer - low

    def get(self, field, layer):
        ref, k = self.find(layer)
        return ref[field, k]

    def put(self, field, layer, value):
        for ref, low, high, start in self.parts:
            if low <= layer < high:
                ref[field, start + layer - low] = value


def facing(own):
    depth = own.shape[1]
    odd = lax.axis_index("gz") % 2
    return depth, odd, (1 - 2 * odd).astype(jnp.float32), Walls(own.shape[2:]), base_speed(own.shape[2:])


def forward_cross_kernel(own, cross, partial, force, first):
    depth, odd, sign, walls, speed = facing(own)

    def at(field, layer):
        return layer_of((cross, own, None), field, layer, depth, odd)

    e = Level((force, -3, 0, 0), (partial, 0, depth - 1, 0))
    one = Level((first, -2, 0, 0), (partial, 0, 2, 3))
    two = Level((partial, -1, 1, 5))
    explicit(at, e.put, range(-3, depth - 1), sign, walls, speed)
    for f in range(4):
        for layer in range(-2, 2):
            one.put(f, layer, (e.get(f, layer) + neighbours(e.get, f, layer, walls)) * SCALE)
        for layer in range(-1, 1):
            two.put(f, layer, (e.get(f, layer) + neighbours(one.get, f, layer, walls)) * SCALE)


def forward_chip_kernel(own, chip, partial, ends, force, first, second):
    depth, odd, sign, walls, speed = facing(own)

    def at(field, layer):
        return layer_of((None, own, chip), field, layer, depth, odd)

    e = Level((partial, 0, depth - 1, 0), (force, depth - 1, depth + 3, 0))
    one = Level((partial, 0, 2, 3), (first, 2, depth + 2, 0))
    two = Level((partial, -1, 1, 5), (second, 1, depth + 1, 0))
    explicit(at, e.put, range(depth - 1, depth + 3), sign, walls, speed)
    for f in range(4):
        for layer in range(2, depth + 2):
            one.put(f, layer, (e.get(f, layer) + neighbours(e.get, f, layer, walls)) * SCALE)
        for layer in range(1, depth + 1):
            two.put(f, layer, (e.get(f, layer) + neighbours(one.get, f, layer, walls)) * SCALE)
        for layer in range(depth):
            total = e.get(f, layer) + neighbours(two.get, f, layer, walls)
            ends[f, place(layer, depth, odd)] = total * SCALE


def turn(field, amount):
    return pltpu.roll(field, amount, 1)


def compare_kernel(shift, ends, following, mismatch):
    fields, depth, rows, columns = ends.shape
    last = lax.axis_index("tm") == lax.axis_size("tm") - 1
    amount = jnp.where(last, shift[0], 0)
    for f in range(fields):
        for k in range(depth):
            mismatch[f, k] = ends[f, k] - turn(following[f, k], amount)


def carry_kernel(shift, own, prior_ends, prior):
    fields, depth, rows, columns = own.shape
    is_first = lax.axis_index("tm") == 0
    amount = jnp.where(is_first, columns - shift[0], 0) % columns
    for f in range(fields):
        for k in range(depth):
            prior[f, k] = turn(prior_ends[f, k], amount) - own[f, k]


def adjoint_cross_kernel(own_mis, cross_mis, partial, first, second):
    depth, odd, sign, walls, speed = facing(own_mis)

    def c(field, layer):
        return layer_of((cross_mis, own_mis, None), field, layer, depth, odd)

    one = Level((first, -3, 1, 0), (partial, 1, 3, 2))
    two = Level((second, -2, 0, 0), (partial, 0, 2, 4))
    for f in range(4):
        for layer in range(-3, 3):
            one.put(f, layer, neighbours(c, f, layer, walls) * SCALE)
        for layer in range(-2, 2):
            two.put(f, layer, neighbours(one.get, f, layer, walls) * SCALE)
        for layer in range(-1, 1):
            last = neighbours(two.get, f, layer, walls)
            partial[f, layer + 1] = (c(f, layer) + one.get(f, layer) + two.get(f, layer) + last) * SCALE


def adjoint_chip_kernel(step_size, own, chip, cross, own_mis, chip_mis, prior, partial, updated, cot, first, second):
    depth, odd, sign, walls, speed = facing(own)

    def at(field, layer):
        return layer_of((cross, own, chip), field, layer, depth, odd)

    def c(field, layer):
        return layer_of((None, own_mis, chip_mis), field, layer, depth, odd)

    one = Level((partial, 1, 3, 2), (first, 3, depth + 3, 0))
    two = Level((partial, 0, 2, 4), (second, 2, depth + 2, 0))
    total = Level((partial, -1, 1, 0), (cot, 1, depth + 1, 0))
    for f in range(4):
        for layer in range(3, depth + 3):
            one.put(f, layer, neighbours(c, f, layer, walls) * SCALE)
        for layer in range(2, depth + 2):
            two.put(f, layer, neighbours(one.get, f, layer, walls) * SCALE)
        for layer in range(1, depth + 1):
            last = neighbours(two.get, f, layer, walls)
            total.put(f, layer, (c(f, layer) + one.get(f, layer) + two.get(f, layer) + last) * SCALE)

    size = step_size[0]
    half = HALF_TAU

    def th(f):
        return lane_up(f) - lane_down(f)

    def rad(f):
        return walls.up(f) - walls.down(f)

    for layer in range(depth):
        here = [at(f, layer) for f in range(4)]
        u, v, w, p = here
        c0, c1, c2, c3 = (total.get(f, layer) for f in range(4))
        below = [total.get(f, layer - 1) for f in range(4)]
        above = [total.get(f, layer + 1) for f in range(4)]
        w_below, w_above = at(2, layer - 1), at(2, layer + 1)
        swirl = speed + v
        pull_r = c0 * rad(u) + c1 * rad(v) + c2 * rad(w)
        pull_th = c0 * th(u) + c1 * th(v) + c2 * th(w)
        pull_z = sum(x * (at(f, layer + 1) - at(f, layer - 1)) for f, x in ((0, c0), (1, c1), (2, c2)))
        axial = [w_above * above[f] - w_below * below[f] for f in range(3)]
        grads = [
            c0 + half * (th(swirl * c0) + rad(u * c0 + c3) + sign * axial[0] - pull_r) - TAU * speed * c1,
            c1
            + half * (th(swirl * c1 + c3) + rad(u * c1) + sign * axial[1] - pull_th)
            + (2.0 * TAU) * speed * c0,
            c2 + half * (th(swirl * c2) + rad(u * c2) + sign * (axial[2] + above[3] - below[3] - pull_z)),
            c3 + half * (rad(c0) + th(c1) + sign * (above[2] - below[2])),
        ]
        to = place(layer, depth, odd)
        for f in range(4):
            updated[f, to] = here[f] - size * (grads[f] - prior[f, to])


def copy_kernel(source, own):
    for f in range(source.shape[0]):
        for k in range(source.shape[1]):
            own[f, k] = source[f, k]


VMEM = pl.BlockSpec(memory_space=pltpu.VMEM)
PARAMS = pltpu.CompilerParams(vmem_limit_bytes=16 * 2**20)
SMEM = pl.BlockSpec(memory_space=pltpu.SMEM)


def kernel(body, like, ins, out_layers, scratch_layers=(), name=None, passes=50):
    fields, depth, rows, columns = like.shape
    size = fields * depth * rows * columns
    return pl.pallas_call(
        body,
        out_shape=jax.ShapeDtypeStruct((fields, out_layers, rows, columns), jnp.float32),
        in_specs=ins,
        out_specs=VMEM,
        scratch_shapes=[pltpu.VMEM((fields, n, rows, columns), jnp.float32) for n in scratch_layers],
        cost_estimate=pl.CostEstimate(flops=passes * size, bytes_accessed=4 * size, transcendentals=0),
        compiler_params=PARAMS,
        name=name,
    )


def per_device(states, shift, step_size):
    start = states[0]
    depth = start.shape[1]
    slabs, sections = lax.axis_size("gz"), lax.axis_size("tm")
    same_chip = [(i, i ^ 1) for i in range(slabs)]
    next_chip = [(i, (i + 1 if i % 2 else i - 1) % slabs) for i in range(slabs)]
    forth = [(i, (i + 1) % sections) for i in range(sections)]
    back = [((i + 1) % sections, i) for i in range(sections)]

    cross = lax.ppermute(start, "gz", next_chip)
    pairs = [[i, i + 1] for i in range(0, slabs, 2)]
    other = 1 - lax.axis_index("gz") % 2
    low = lax.all_gather(start[:2], "gz", axis_index_groups=pairs)
    high = lax.all_gather(start[2:], "gz", axis_index_groups=pairs)
    chip = jnp.concatenate([low[other], high[other]])
    following = lax.ppermute(start, "tm", back)
    own = kernel(copy_kernel, start, [VMEM], depth, name="stage")(start)
    partial = kernel(forward_cross_kernel, start, [VMEM] * 2, 7, (3, 2), "forward_cross")(own, cross)
    ends = kernel(forward_chip_kernel, start, [VMEM] * 3, depth, (4, 4, 4), "forward_chip")(own, chip, partial)
    ends, following = lax.optimization_barrier((ends, following))
    prior_ends = lax.ppermute(ends, "tm", forth)
    mismatch = kernel(compare_kernel, start, [SMEM, VMEM, VMEM], depth, (), "compare")(shift, ends, following)
    cross_mis = lax.ppermute(mismatch, "gz", next_chip)
    chip_mis = lax.ppermute(mismatch, "gz", same_chip)
    prior = kernel(carry_kernel, start, [SMEM, VMEM, VMEM], depth, (), "carry", 2)(shift, own, prior_ends)
    partial = kernel(adjoint_cross_kernel, start, [VMEM] * 2, 6, (4, 2), "adjoint_cross")(mismatch, cross_mis)
    updated = kernel(adjoint_chip_kernel, start, [SMEM] + [VMEM] * 7, depth, (4, 4, 4), "adjoint_chip")(
        step_size, own, chip, cross, mismatch, chip_mis, prior, partial
    )
    shown = kernel(copy_kernel, start, [VMEM], depth, name="publish")(mismatch)
    return updated[None], shown[None]


def solution(mesh):
    placed = P("tm", None, "gz", None, None)
    return jax.shard_map(
        per_device,
        mesh=mesh,
        in_specs=(placed, P(), P()),
        out_specs=(placed, placed),
        check_vma=False,
    )
```

time: 66.1 us -> 55.1 us (0.83)
  the two profiles are of different devices: /device:TPU:2 before, /device:TPU:1 now
where the time goes in v2:
time: 55.1 us; the launch traced here: 54.2 us
  starting transfers between devices  25.6 us (46%)
  blocking collectives  11.5 us (21%)
  Pallas kernels  7.29 us (13%)
  waiting for transfers between devices  6.49 us (12%)
  between operations  2.08 us (4%)
  local copies, waits for them, and re-layouts  1.12 us (2%)
    all_gather x1, blocking collectives, per_device(): high = lax.all_gather(start[2:], 'gz', axis_index_groups=pairs)  9.36 us
    ppermute x1, starting transfers between devices, per_device(): chip_mis = lax.ppermute(mismatch, 'gz', same_chip)  8.85 us
    ppermute x1, starting transfers between devices, per_device(): following = lax.ppermute(start, 'tm', back)  7.56 us
    ppermute x1, waiting for transfers between devices, per_device(): prior_ends = lax.ppermute(ends, 'tm', forth)  6.48 us
    ppermute x1, starting transfers between devices, per_device(): cross = lax.ppermute(start, 'gz', next_chip)  5.39 us
    pallas_call x1, Pallas kernels, per_device(): kernel(adjoint_chip_kernel, start, [SMEM] + [VMEM] * 7, depth, (4, 4, 4),...  2.46 us
    all_gather x1, blocking collectives, per_device(): low = lax.all_gather(start[:2], 'gz', axis_index_groups=pairs)  2.18 us
    ppermute x1, starting transfers between devices, per_device(): prior_ends = lax.ppermute(ends, 'tm', forth)  1.92 us
  transfers between devices with their start and end apart: 5, of which 1 were waited for; matrix products, arithmetic and copies ran while one was open for 2% of the time, Pallas kernels for 9%

profile of v2, /device:TPU:1, one launch (start us, length us, event | category | flops | bytes accessed | tf_op | source)
XLA Modules:
  0.0 54.2 jit_solution(7237297924548924368)
XLA Ops:
  0.6 5.4 %collective-permute-start = (f32[4,4,64,128]{3,2,1,0:T(8,128)}, f32[4,4,64,128]{3,2,1,0:T(8,128)S(1)}, u32[]{:S(2)}, u32[]{:S(2)}) collective-permute-start(f32[4,4,64,128]{3,2,1,0:T(8,128)} %bitcast.7), channel_id=1, source_target_pairs={{0,31},{1,2},{2,1},{3,4},{4,3},{5,6},{6,5},{7,8},{8,7},{9,10},{10,... | collective-permute-start | bytes 1572872 | tf_op jit(solution)/shard_map/ppermute | solution.py:272
  6.0 7.6 %collective-permute-start.1 = (f32[4,4,64,128]{3,2,1,0:T(8,128)}, f32[4,4,64,128]{3,2,1,0:T(8,128)S(1)}, u32[]{:S(2)}, u32[]{:S(2)}) collective-permute-start(f32[4,4,64,128]{3,2,1,0:T(8,128)} %bitcast.8), channel_id=1, source_target_pairs={{32,0},{64,32},{96,64},{128,96},{160,128},{192,160},{224,192},{256... | collective-permute-start | bytes 1572872 | tf_op jit(solution)/shard_map/ppermute | solution.py:278
  13.6 1.1 %fusion = (f32[1,2,4,64,128]{4,3,2,1,0:T(8,128)S(1)}, f32[1,2,4,64,128]{4,3,2,1,0:T(8,128)S(1)}) fusion(f32[1,4,4,64,128]{4,3,2,1,0:T(8,128)} %param.3), kind=kLoop, calls=%fused_computation.3 | loop fusion | bytes 1048576 | tf_op jit(solution)/shard_map/slice | solution.py:275
  14.7 0.0 copy-start
  14.7 9.4 %all_gather.9 = f32[2,2,4,64,128]{4,3,2,1,0:T(8,128)S(1)} all-gather(f32[1,2,4,64,128]{4,3,2,1,0:T(8,128)S(1)} %get-tuple-element.7), channel_id=1, replica_groups={{0,1},{2,3},{4,5},{6,7},{8,9},{10,11},{12,13},{14,15},{16,17},{18,19},{..., dimensions={0}, use_global_device_ids=true | all-gather | bytes 786432 | tf_op jit(solution)/shard_map/all_gather | solution.py:276
  24.7 0.0 copy-done
  24.8 2.2 %all_gather.8 = f32[2,2,4,64,128]{4,3,2,1,0:T(8,128)S(1)} all-gather(f32[1,2,4,64,128]{4,3,2,1,0:T(8,128)S(1)} %get-tuple-element.6), channel_id=1, replica_groups={{0,1},{2,3},{4,5},{6,7},{8,9},{10,11},{12,13},{14,15},{16,17},{18,19},{..., dimensions={0}, use_global_device_ids=true | all-gather | bytes 786432 | tf_op jit(solution)/shard_map/all_gather | solution.py:275
  27.0 0.0 collective-permute-done.cross
  27.0 1.1 %forward_cross.1.partial = f32[4,7,64,128]{3,2,1,0:T(8,128)S(1)} custom-call(f32[4,4,64,128]{3,2,1,0:T(8,128)S(1)} %stage.1.own, f32[4,4,64,128]{3,2,1,0:T(8,128)S(1)} %collective-permute-done.cross), custom_call_target="tpu_custom_call" | custom-call | flops 6553600 | bytes 524288 | tf_op jit(solution)/shard_map/forward_cross/pallas_call | solution.py:280
  28.2 1.3 %forward_chip.1.ends = f32[4,4,64,128]{3,2,1,0:T(8,128)S(1)} custom-call(f32[4,4,64,128]{3,2,1,0:T(8,128)S(1)} %stage.1.own, f32[4,4,64,128]{3,2,1,0:T(8,128)S(1)} %pad_maximum_fusion.chip, f32[4,7,64,128]{3,2,1,0:T(8,128)S(1)} %forward_cross.1.partial), custom_call_target="tpu_custom_call" | custom-call | flops 6553600 | bytes 524288 | tf_op jit(solution)/shard_map/forward_chip/pallas_call | solution.py:281
  29.5 0.0 collective-permute-done.1.following
  29.5 1.9 %collective-permute-start.3 = (f32[4,4,64,128]{3,2,1,0:T(8,128)S(1)}, f32[4,4,64,128]{3,2,1,0:T(8,128)S(1)}, u32[]{:S(2)}, u32[]{:S(2)}) collective-permute-start(f32[4,4,64,128]{3,2,1,0:T(8,128)S(1)} %forward_chip.1.ends), channel_id=1, source_target_pairs={{0,32},{32,64},{64,96},{96,128},{128,160},{160,192},{192,224},{224... | collective-permute-start | bytes 1572872 | tf_op jit(solution)/shard_map/ppermute | solution.py:283
  31.5 0.2 compare.2.own_mis.source
  31.7 1.9 %collective-permute-start.4 = (f32[4,4,64,128]{3,2,1,0:T(8,128)S(1)}, f32[4,4,64,128]{3,2,1,0:T(8,128)S(1)}, u32[]{:S(2)}, u32[]{:S(2)}) collective-permute-start(f32[4,4,64,128]{3,2,1,0:T(8,128)S(1)} %compare.2.own_mis.source), channel_id=1, source_target_pairs={{0,31},{1,2},{2,1},{3,4},{4,3},{5,6},{6,5},{7,8},{8,7},{9,10},{10,... | collective-permute-start | bytes 1572872 | tf_op jit(solution)/shard_map/ppermute | solution.py:285
  33.6 8.8 %collective-permute-start.2 = (f32[4,4,64,128]{3,2,1,0:T(8,128)S(1)}, f32[4,4,64,128]{3,2,1,0:T(8,128)S(1)}, u32[]{:S(2)}, u32[]{:S(2)}) collective-permute-start(f32[4,4,64,128]{3,2,1,0:T(8,128)S(1)} %compare.2.own_mis.source), channel_id=1, source_target_pairs={{0,1},{1,0},{2,3},{3,2},{4,5},{5,4},{6,7},{7,6},{8,9},{9,8},{10,11... | collective-permute-start | bytes 1572872 | tf_op jit(solution)/shard_map/ppermute | solution.py:286
  43.1 0.8 %publish.1 = f32[4,4,64,128]{3,2,1,0:T(8,128)} custom-call(f32[4,4,64,128]{3,2,1,0:T(8,128)S(1)} %compare.2.own_mis.source), custom_call_target="tpu_custom_call" | custom-call | flops 6553600 | bytes 524288 | tf_op jit(solution)/shard_map/publish/pallas_call | solution.py:292
  43.9 6.5 %collective-permute-done.3.prior_ends = f32[4,4,64,128]{3,2,1,0:T(8,128)S(1)} collective-permute-done((f32[4,4,64,128]{3,2,1,0:T(8,128)S(1)}, f32[4,4,64,128]{3,2,1,0:T(8,128)S(1)}, u32[]{:S(2)}, u32[]{:S(2)}) %collective-permute-start.3) | collective-permute-done | bytes 524320 | tf_op jit(solution)/shard_map/ppermute | solution.py:283
  50.4 0.2 carry.1.prior
  50.6 0.0 collective-permute-done.4.cross_mis
  50.6 1.1 %adjoint_cross.1.partial = f32[4,6,64,128]{3,2,1,0:T(8,128)S(1)} custom-call(f32[4,4,64,128]{3,2,1,0:T(8,128)S(1)} %compare.2.own_mis.source, f32[4,4,64,128]{3,2,1,0:T(8,128)S(1)} %collective-permute-done.4.cross_mis), custom_call_target="tpu_custom_call" | custom-call | flops 6553600 | bytes 524288 | tf_op jit(solution)/shard_map/adjoint_cross/pallas_call | solution.py:288
  51.7 0.0 collective-permute-done.2.chip_mis
  51.7 2.5 %adjoint_chip.1 = f32[4,4,64,128]{3,2,1,0:T(8,128)} custom-call(f32[1]{0:T(128)S(6)} %copy.6.step_size, f32[4,4,64,128]{3,2,1,0:T(8,128)S(1)} %stage.1.own, f32[4,4,64,128]{3,2,1,0:T(8,128)S(1)} %pad_maximum_fusion.chip, f32[4,4,64,128]{3,2,1,0:T(8,128)S(1)} %collective-permute-done.cross, f32[4,4,64,128]{3,2,1,0:T(8,128)S(1)} %compare.2.own_mis.source, ...), custom_call_target="tpu_custom_call" | custom-call | flops 6553600 | bytes 524288 | tf_op jit(solution)/shard_map/adjoint_chip/pallas_call | solution.py:289
  (4 shorter events, 0.1 us)
Async XLA Ops:
  0.6 26.4 %collective-permute-start = (f32[4,4,64,128]{3,2,1,0:T(8,128)}, f32[4,4,64,128]{3,2,1,0:T(8,128)S(1)}, u32[]{:S(2)}, u32[]{:S(2)}) collective-permute-start(f32[4,4,64,128]{3,2,1,0:T(8,128)} %bitcast.7), channel_id=1, source_target_pairs={{0,31},{1,2},{2,1},{3,4},{4,3},{5,6},{6,5},{7,8},{8,7},{9,10},{10,... | collective-permute-start | bytes 1572872 | tf_op jit(solution)/shard_map/ppermute | solution.py:272
  6.0 23.5 %collective-permute-start.1 = (f32[4,4,64,128]{3,2,1,0:T(8,128)}, f32[4,4,64,128]{3,2,1,0:T(8,128)S(1)}, u32[]{:S(2)}, u32[]{:S(2)}) collective-permute-start(f32[4,4,64,128]{3,2,1,0:T(8,128)} %bitcast.8), channel_id=1, source_target_pairs={{32,0},{64,32},{96,64},{128,96},{160,128},{192,160},{224,192},{256... | collective-permute-start | bytes 1572872 | tf_op jit(solution)/shard_map/ppermute | solution.py:278
  14.7 10.0 %copy-start = (f32[1,4,4,64,128]{4,3,2,1,0:T(8,128)S(1)}, f32[1,4,4,64,128]{4,3,2,1,0:T(8,128)}, u32[]{:S(2)}) copy-start(f32[1,4,4,64,128]{4,3,2,1,0:T(8,128)} %param.3) | copy-start | bytes 1572868
  29.5 20.9 %collective-permute-start.3 = (f32[4,4,64,128]{3,2,1,0:T(8,128)S(1)}, f32[4,4,64,128]{3,2,1,0:T(8,128)S(1)}, u32[]{:S(2)}, u32[]{:S(2)}) collective-permute-start(f32[4,4,64,128]{3,2,1,0:T(8,128)S(1)} %forward_chip.1.ends), channel_id=1, source_target_pairs={{0,32},{32,64},{64,96},{96,128},{128,160},{160,192},{192,224},{224... | collective-permute-start | bytes 1572872 | tf_op jit(solution)/shard_map/ppermute | solution.py:283
  31.7 19.0 %collective-permute-start.4 = (f32[4,4,64,128]{3,2,1,0:T(8,128)S(1)}, f32[4,4,64,128]{3,2,1,0:T(8,128)S(1)}, u32[]{:S(2)}, u32[]{:S(2)}) collective-permute-start(f32[4,4,64,128]{3,2,1,0:T(8,128)S(1)} %compare.2.own_mis.source), channel_id=1, source_target_pairs={{0,31},{1,2},{2,1},{3,4},{4,3},{5,6},{6,5},{7,8},{8,7},{9,10},{10,... | collective-permute-start | bytes 1572872 | tf_op jit(solution)/shard_map/ppermute | solution.py:285
  33.6 18.1 %collective-permute-start.2 = (f32[4,4,64,128]{3,2,1,0:T(8,128)S(1)}, f32[4,4,64,128]{3,2,1,0:T(8,128)S(1)}, u32[]{:S(2)}, u32[]{:S(2)}) collective-permute-start(f32[4,4,64,128]{3,2,1,0:T(8,128)S(1)} %compare.2.own_mis.source), channel_id=1, source_target_pairs={{0,1},{1,0},{2,3},{3,2},{4,5},{5,4},{6,7},{7,6},{8,9},{9,8},{10,11... | collective-permute-start | bytes 1572872 | tf_op jit(solution)/shard_map/ppermute | solution.py:286

commit v3 on v2

--- a/solution.py
+++ b/solution.py
@@ -73,32 +73,67 @@
         put(3, layer, p - HALF_TAU * (d_r[0] + d_th[1] + sign * d_z[2]))
 
 
-def neighbours(at, field, layer, walls):
-    return at(field, layer - 1) + at(field, layer + 1) + in_plane(at(field, layer), walls)
+PAD = 8
+
+
+class Slabs:
+    def __init__(self, refs, depth, odd, walls):
+        self.refs, self.depth, self.odd, self.walls = refs, depth, odd, walls
+
+    def get(self, field, layer):
+        return layer_of(self.refs, field, layer, self.depth, self.odd)
+
+    def up(self, field, layer):
+        return self.walls.up(self.get(field, layer))
+
+    def down(self, field, layer):
+        return self.walls.down(self.get(field, layer))
 
 
 class Level:
     def __init__(self, *parts):
         self.parts = parts
-
-    def find(self, layer):
+        self.rows = parts[0][0].shape[2] - 2 * PAD
+
+    def at(self, field, layer, first):
         for ref, low, high, start in self.parts:
             if low <= layer < high:
-                return ref, start + layer - low
+                return ref[field, start + layer - low, first : first + self.rows]
 
     def get(self, field, layer):
-        ref, k = self.find(layer)
-        return ref[field, k]
+        return self.at(field, layer, PAD)
+
+    def up(self, field, layer):
+        return self.at(field, layer, PAD + 1)
+
+    def down(self, field, layer):
+        return self.at(field, layer, PAD - 1)
 
     def put(self, field, layer, value):
         for ref, low, high, start in self.parts:
             if low <= layer < high:
-                ref[field, start + layer - low] = value
-
-
-def facing(own):
+                ref[field, start + layer - low, PAD : PAD + self.rows] = value
+
+
+def clear_pads(*refs):
+    for ref in refs:
+        fields, layers, rows, columns = ref.shape
+        nothing = jnp.zeros((PAD, columns), jnp.float32)
+        for f in range(fields):
+            for k in range(layers):
+                ref[f, k, :PAD] = nothing
+                ref[f, k, rows - PAD :] = nothing
+
+
+def neighbours(level, field, layer):
+    here = level.get(field, layer)
+    around = level.get(field, layer - 1) + level.get(field, layer + 1) + lane_up(here) + lane_down(here)
+    return around + level.up(field, layer) + level.down(field, layer)
+
+
+def facing(own, turned=0):
     depth = own.shape[1]
-    odd = lax.axis_index("gz") % 2
+    odd = (lax.axis_index("gz") + turned) % 2
     return depth, odd, (1 - 2 * odd).astype(jnp.float32), Walls(own.shape[2:]), base_speed(own.shape[2:])
 
 
@@ -108,15 +143,16 @@
     def at(field, layer):
         return layer_of((cross, own, None), field, layer, depth, odd)
 
+    clear_pads(partial, force, first)
     e = Level((force, -3, 0, 0), (partial, 0, depth - 1, 0))
     one = Level((first, -2, 0, 0), (partial, 0, 2, 3))
     two = Level((partial, -1, 1, 5))
     explicit(at, e.put, range(-3, depth - 1), sign, walls, speed)
     for f in range(4):
         for layer in range(-2, 2):
-            one.put(f, layer, (e.get(f, layer) + neighbours(e.get, f, layer, walls)) * SCALE)
+            one.put(f, layer, (e.get(f, layer) + neighbours(e, f, layer)) * SCALE)
         for layer in range(-1, 1):
-            two.put(f, layer, (e.get(f, layer) + neighbours(one.get, f, layer, walls)) * SCALE)
+            two.put(f, layer, (e.get(f, layer) + neighbours(one, f, layer)) * SCALE)
 
 
 def forward_chip_kernel(own, chip, partial, ends, force, first, second):
@@ -125,17 +161,18 @@
     def at(field, layer):
         return layer_of((None, own, chip), field, layer, depth, odd)
 
+    clear_pads(force, first, second)
     e = Level((partial, 0, depth - 1, 0), (force, depth - 1, depth + 3, 0))
     one = Level((partial, 0, 2, 3), (first, 2, depth + 2, 0))
     two = Level((partial, -1, 1, 5), (second, 1, depth + 1, 0))
     explicit(at, e.put, range(depth - 1, depth + 3), sign, walls, speed)
     for f in range(4):
         for layer in range(2, depth + 2):
-            one.put(f, layer, (e.get(f, layer) + neighbours(e.get, f, layer, walls)) * SCALE)
+            one.put(f, layer, (e.get(f, layer) + neighbours(e, f, layer)) * SCALE)
         for layer in range(1, depth + 1):
-            two.put(f, layer, (e.get(f, layer) + neighbours(one.get, f, layer, walls)) * SCALE)
+            two.put(f, layer, (e.get(f, layer) + neighbours(one, f, layer)) * SCALE)
         for layer in range(depth):
-            total = e.get(f, layer) + neighbours(two.get, f, layer, walls)
+            total = e.get(f, layer) + neighbours(two, f, layer)
             ends[f, place(layer, depth, odd)] = total * SCALE
 
 
@@ -161,44 +198,45 @@
             prior[f, k] = turn(prior_ends[f, k], amount) - own[f, k]
 
 
-def adjoint_cross_kernel(own_mis, cross_mis, partial, first, second):
-    depth, odd, sign, walls, speed = facing(own_mis)
-
-    def c(field, layer):
-        return layer_of((cross_mis, own_mis, None), field, layer, depth, odd)
-
+def adjoint_chip_kernel(own_mis, chip_mis, partial, first, second):
+    depth, odd, sign, walls, speed = facing(own_mis, 1)
+
+    c = Slabs((chip_mis, own_mis, None), depth, odd, walls)
+
+    clear_pads(partial, first, second)
     one = Level((first, -3, 1, 0), (partial, 1, 3, 2))
     two = Level((second, -2, 0, 0), (partial, 0, 2, 4))
+    total = Level((partial, -1, 1, 0))
     for f in range(4):
         for layer in range(-3, 3):
-            one.put(f, layer, neighbours(c, f, layer, walls) * SCALE)
+            one.put(f, layer, neighbours(c, f, layer) * SCALE)
         for layer in range(-2, 2):
-            two.put(f, layer, neighbours(one.get, f, layer, walls) * SCALE)
+            two.put(f, layer, neighbours(one, f, layer) * SCALE)
         for layer in range(-1, 1):
-            last = neighbours(two.get, f, layer, walls)
-            partial[f, layer + 1] = (c(f, layer) + one.get(f, layer) + two.get(f, layer) + last) * SCALE
-
-
-def adjoint_chip_kernel(step_size, own, chip, cross, own_mis, chip_mis, prior, partial, updated, cot, first, second):
-    depth, odd, sign, walls, speed = facing(own)
+            last = neighbours(two, f, layer)
+            total.put(f, layer, (c.get(f, layer) + one.get(f, layer) + two.get(f, layer) + last) * SCALE)
+
+
+def adjoint_cross_kernel(step_size, own, chip, cross, own_mis, cross_mis, prior, partial, updated, cot, first, second):
+    depth, odd, sign, walls, speed = facing(own, 1)
 
     def at(field, layer):
-        return layer_of((cross, own, chip), field, layer, depth, odd)
-
-    def c(field, layer):
-        return layer_of((None, own_mis, chip_mis), field, layer, depth, odd)
-
+        return layer_of((chip, own, cross), field, layer, depth, odd)
+
+    c = Slabs((None, own_mis, cross_mis), depth, odd, walls)
+
+    clear_pads(cot, first, second)
     one = Level((partial, 1, 3, 2), (first, 3, depth + 3, 0))
     two = Level((partial, 0, 2, 4), (second, 2, depth + 2, 0))
     total = Level((partial, -1, 1, 0), (cot, 1, depth + 1, 0))
     for f in range(4):
         for layer in range(3, depth + 3):
-            one.put(f, layer, neighbours(c, f, layer, walls) * SCALE)
+            one.put(f, layer, neighbours(c, f, layer) * SCALE)
         for layer in range(2, depth + 2):
-            two.put(f, layer, neighbours(one.get, f, layer, walls) * SCALE)
+            two.put(f, layer, neighbours(one, f, layer) * SCALE)
         for layer in range(1, depth + 1):
-            last = neighbours(two.get, f, layer, walls)
-            total.put(f, layer, (c(f, layer) + one.get(f, layer) + two.get(f, layer) + last) * SCALE)
+            last = neighbours(two, f, layer)
+            total.put(f, layer, (c.get(f, layer) + one.get(f, layer) + two.get(f, layer) + last) * SCALE)
 
     size = step_size[0]
     half = HALF_TAU
@@ -227,7 +265,7 @@
             + half * (th(swirl * c1 + c3) + rad(u * c1) + sign * axial[1] - pull_th)
             + (2.0 * TAU) * speed * c0,
             c2 + half * (th(swirl * c2) + rad(u * c2) + sign * (axial[2] + above[3] - below[3] - pull_z)),
-            c3 + half * (rad(c0) + th(c1) + sign * (above[2] - below[2])),
+            c3 + half * (total.up(0, layer) - total.down(0, layer) + th(c1) + sign * (above[2] - below[2])),
         ]
         to = place(layer, depth, odd)
         for f in range(4):
@@ -245,15 +283,15 @@
 SMEM = pl.BlockSpec(memory_space=pltpu.SMEM)
 
 
-def kernel(body, like, ins, out_layers, scratch_layers=(), name=None, passes=50):
+def kernel(body, like, ins, out_layers, scratch_layers=(), name=None, passes=50, pad=0):
     fields, depth, rows, columns = like.shape
     size = fields * depth * rows * columns
     return pl.pallas_call(
         body,
-        out_shape=jax.ShapeDtypeStruct((fields, out_layers, rows, columns), jnp.float32),
+        out_shape=jax.ShapeDtypeStruct((fields, out_layers, rows + 2 * pad, columns), jnp.float32),
         in_specs=ins,
         out_specs=VMEM,
-        scratch_shapes=[pltpu.VMEM((fields, n, rows, columns), jnp.float32) for n in scratch_layers],
+        scratch_shapes=[pltpu.VMEM((fields, n, rows + 2 * PAD, columns), jnp.float32) for n in scratch_layers],
         cost_estimate=pl.CostEstimate(flops=passes * size, bytes_accessed=4 * size, transcendentals=0),
         compiler_params=PARAMS,
         name=name,
@@ -264,7 +302,6 @@
     start = states[0]
     depth = start.shape[1]
     slabs, sections = lax.axis_size("gz"), lax.axis_size("tm")
-    same_chip = [(i, i ^ 1) for i in range(slabs)]
     next_chip = [(i, (i + 1 if i % 2 else i - 1) % slabs) for i in range(slabs)]
     forth = [(i, (i + 1) % sections) for i in range(sections)]
     back = [((i + 1) % sections, i) for i in range(sections)]
@@ -277,17 +314,19 @@
     chip = jnp.concatenate([low[other], high[other]])
     following = lax.ppermute(start, "tm", back)
     own = kernel(copy_kernel, start, [VMEM], depth, name="stage")(start)
-    partial = kernel(forward_cross_kernel, start, [VMEM] * 2, 7, (3, 2), "forward_cross")(own, cross)
+    partial = kernel(forward_cross_kernel, start, [VMEM] * 2, 7, (3, 2), "forward_cross", pad=PAD)(own, cross)
     ends = kernel(forward_chip_kernel, start, [VMEM] * 3, depth, (4, 4, 4), "forward_chip")(own, chip, partial)
     ends, following = lax.optimization_barrier((ends, following))
     prior_ends = lax.ppermute(ends, "tm", forth)
     mismatch = kernel(compare_kernel, start, [SMEM, VMEM, VMEM], depth, (), "compare")(shift, ends, following)
     cross_mis = lax.ppermute(mismatch, "gz", next_chip)
-    chip_mis = lax.ppermute(mismatch, "gz", same_chip)
+    low = lax.all_gather(mismatch[:2], "gz", axis_index_groups=pairs)
+    high = lax.all_gather(mismatch[2:], "gz", axis_index_groups=pairs)
+    chip_mis = jnp.concatenate([low[other], high[other]])
     prior = kernel(carry_kernel, start, [SMEM, VMEM, VMEM], depth, (), "carry", 2)(shift, own, prior_ends)
-    partial = kernel(adjoint_cross_kernel, start, [VMEM] * 2, 6, (4, 2), "adjoint_cross")(mismatch, cross_mis)
-    updated = kernel(adjoint_chip_kernel, start, [SMEM] + [VMEM] * 7, depth, (4, 4, 4), "adjoint_chip")(
-        step_size, own, chip, cross, mismatch, chip_mis, prior, partial
+    partial = kernel(adjoint_chip_kernel, start, [VMEM] * 2, 6, (4, 2), "adjoint_chip", pad=PAD)(mismatch, chip_mis)
+    updated = kernel(adjoint_cross_kernel, start, [SMEM] + [VMEM] * 7, depth, (4, 4, 4), "adjoint_cross")(
+        step_size, own, chip, cross, mismatch, cross_mis, prior, partial
     )
     shown = kernel(copy_kernel, start, [VMEM], depth, name="publish")(mismatch)
     return updated[None], shown[None]

time: 55.1 us -> 54.9 us (level); the launches traced: 54.2 us -> 54.6 us
  blocking collectives: 11.5 us -> 21.9 us
  starting transfers between devices: 25.6 us -> 16.9 us
  waiting for transfers between devices: 6.49 us -> 5.39 us
    all_gather x0 -> x2, blocking collectives: none -> 10.5 us  [the longest x1 8.36 us: per_device(): high = lax.all_gather(mismatch[2:], 'gz', axis_index_groups=pairs)]
    ppermute x1 -> x0, starting transfers between devices: 8.85 us -> none  [per_device(): chip_mis = lax.ppermute(mismatch, 'gz', same_chip)]
    ppermute x1, waiting for transfers between devices: 6.48 us -> 5.38 us  [per_device(): prior_ends = lax.ppermute(ends, 'tm', forth)]
  transfers between devices with their start and end apart: 5 -> 4, of which waited for: 1 -> 1; matrix products, arithmetic and copies ran while one was open for 2% -> 2% of each run, Pallas kernels for 9% -> 9%
where the time goes in v3:
time: 54.9 us; the launch traced here: 54.6 us
  blocking collectives  21.9 us (40%)
  starting transfers between devices  16.9 us (31%)
  Pallas kernels  6.95 us (13%)
  waiting for transfers between devices  5.39 us (10%)
  between operations  2.09 us (4%)
  local copies, waits for them, and re-layouts  1.19 us (2%)
    all_gather x1, blocking collectives, per_device(): high = lax.all_gather(start[2:], 'gz', axis_index_groups=pairs)  9.22 us
    all_gather x1, blocking collectives, per_device(): high = lax.all_gather(mismatch[2:], 'gz', axis_index_groups=pairs)  8.36 us
    ppermute x1, starting transfers between devices, per_device(): following = lax.ppermute(start, 'tm', back)  7.56 us
    ppermute x1, starting transfers between devices, per_device(): cross = lax.ppermute(start, 'gz', next_chip)  5.52 us
    ppermute x1, waiting for transfers between devices, per_device(): prior_ends = lax.ppermute(ends, 'tm', forth)  5.38 us
    pallas_call x1, Pallas kernels, per_device(): kernel(adjoint_cross_kernel, start, [SMEM] + [VMEM] * 7, depth, (4, 4, 4)...  2.28 us
    all_gather x1, blocking collectives, per_device(): low = lax.all_gather(start[:2], 'gz', axis_index_groups=pairs)  2.18 us
    all_gather x1, blocking collectives, per_device(): low = lax.all_gather(mismatch[:2], 'gz', axis_index_groups=pairs)  2.18 us
  transfers between devices with their start and end apart: 4, of which 1 were waited for; matrix products, arithmetic and copies ran while one was open for 2% of the time, Pallas kernels for 9%

profile of v3, /device:TPU:1, one launch (start us, length us, event | category | flops | bytes accessed | tf_op | source)
XLA Modules:
  0.0 54.6 jit_solution(17773970735921864120)
XLA Ops:
  0.6 0.0 copy-start
  0.6 5.5 %collective-permute-start = (f32[4,4,64,128]{3,2,1,0:T(8,128)}, f32[4,4,64,128]{3,2,1,0:T(8,128)S(1)}, u32[]{:S(2)}, u32[]{:S(2)}) collective-permute-start(f32[4,4,64,128]{3,2,1,0:T(8,128)} %bitcast.13), channel_id=1, source_target_pairs={{0,31},{1,2},{2,1},{3,4},{4,3},{5,6},{6,5},{7,8},{8,7},{9,10},{10,... | collective-permute-start | bytes 1572872 | tf_op jit(solution)/shard_map/ppermute | solution.py:309
  6.2 7.6 %collective-permute-start.1 = (f32[4,4,64,128]{3,2,1,0:T(8,128)}, f32[4,4,64,128]{3,2,1,0:T(8,128)S(1)}, u32[]{:S(2)}, u32[]{:S(2)}) collective-permute-start(f32[4,4,64,128]{3,2,1,0:T(8,128)} %bitcast.14), channel_id=1, source_target_pairs={{32,0},{64,32},{96,64},{128,96},{160,128},{192,160},{224,192},{256... | collective-permute-start | bytes 1572872 | tf_op jit(solution)/shard_map/ppermute | solution.py:315
  13.7 1.1 %fusion.1 = (f32[1,2,4,64,128]{4,3,2,1,0:T(8,128)S(1)}, f32[1,2,4,64,128]{4,3,2,1,0:T(8,128)S(1)}) fusion(f32[1,4,4,64,128]{4,3,2,1,0:T(8,128)} %param.3), kind=kLoop, calls=%fused_computation.7 | loop fusion | bytes 1048576 | tf_op jit(solution)/shard_map/slice | solution.py:312
  14.8 9.2 %all_gather.21 = f32[2,2,4,64,128]{4,3,2,1,0:T(8,128)S(1)} all-gather(f32[1,2,4,64,128]{4,3,2,1,0:T(8,128)S(1)} %get-tuple-element.9), channel_id=1, replica_groups={{0,1},{2,3},{4,5},{6,7},{8,9},{10,11},{12,13},{14,15},{16,17},{18,19},{..., dimensions={0}, use_global_device_ids=true | all-gather | bytes 786432 | tf_op jit(solution)/shard_map/all_gather | solution.py:313
  25.3 0.0 copy-done
  25.4 2.2 %all_gather.20 = f32[2,2,4,64,128]{4,3,2,1,0:T(8,128)S(1)} all-gather(f32[1,2,4,64,128]{4,3,2,1,0:T(8,128)S(1)} %get-tuple-element.8), channel_id=1, replica_groups={{0,1},{2,3},{4,5},{6,7},{8,9},{10,11},{12,13},{14,15},{16,17},{18,19},{..., dimensions={0}, use_global_device_ids=true | all-gather | bytes 786432 | tf_op jit(solution)/shard_map/all_gather | solution.py:312
  27.7 0.0 collective-permute-done.cross
  27.7 1.1 %forward_cross.1.partial = f32[4,7,80,128]{3,2,1,0:T(8,128)S(1)} custom-call(f32[4,4,64,128]{3,2,1,0:T(8,128)S(1)} %stage.1.own, f32[4,4,64,128]{3,2,1,0:T(8,128)S(1)} %collective-permute-done.cross), custom_call_target="tpu_custom_call" | custom-call | flops 6553600 | bytes 524288 | tf_op jit(solution)/shard_map/forward_cross/pallas_call | solution.py:317
  28.8 1.2 %forward_chip.1.ends = f32[4,4,64,128]{3,2,1,0:T(8,128)S(1)} custom-call(f32[4,4,64,128]{3,2,1,0:T(8,128)S(1)} %stage.1.own, f32[4,4,64,128]{3,2,1,0:T(8,128)S(1)} %pad_maximum_fusion.chip, f32[4,7,80,128]{3,2,1,0:T(8,128)S(1)} %forward_cross.1.partial), custom_call_target="tpu_custom_call" | custom-call | flops 6553600 | bytes 524288 | tf_op jit(solution)/shard_map/forward_chip/pallas_call | solution.py:318
  30.0 0.0 collective-permute-done.1.following
  30.1 1.9 %collective-permute-start.3 = (f32[4,4,64,128]{3,2,1,0:T(8,128)S(1)}, f32[4,4,64,128]{3,2,1,0:T(8,128)S(1)}, u32[]{:S(2)}, u32[]{:S(2)}) collective-permute-start(f32[4,4,64,128]{3,2,1,0:T(8,128)S(1)} %forward_chip.1.ends), channel_id=1, source_target_pairs={{0,32},{32,64},{64,96},{96,128},{128,160},{160,192},{192,224},{224... | collective-permute-start | bytes 1572872 | tf_op jit(solution)/shard_map/ppermute | solution.py:320
  32.0 0.2 compare.2.own_mis.source
  32.3 1.9 %collective-permute-start.2 = (f32[4,4,64,128]{3,2,1,0:T(8,128)S(1)}, f32[4,4,64,128]{3,2,1,0:T(8,128)S(1)}, u32[]{:S(2)}, u32[]{:S(2)}) collective-permute-start(f32[4,4,64,128]{3,2,1,0:T(8,128)S(1)} %compare.2.own_mis.source), channel_id=1, source_target_pairs={{0,31},{1,2},{2,1},{3,4},{4,3},{5,6},{6,5},{7,8},{8,7},{9,10},{10,... | collective-permute-start | bytes 1572872 | tf_op jit(solution)/shard_map/ppermute | solution.py:322
  34.2 8.4 %all-gather.1 = f32[4,4,64,128]{3,2,1,0:T(8,128)S(1)} all-gather(f32[2,4,64,128]{3,2,1,0:T(8,128)S(1)} %get-tuple-element.7), channel_id=3, replica_groups={{0,1},{2,3},{4,5},{6,7},{8,9},{10,11},{12,13},{14,15},{16,17},{18,19},{..., dimensions={0}, use_global_device_ids=true | all-gather | bytes 786432 | tf_op jit(solution)/shard_map/all_gather | solution.py:324
  42.5 0.8 %publish.1 = f32[4,4,64,128]{3,2,1,0:T(8,128)} custom-call(f32[4,4,64,128]{3,2,1,0:T(8,128)S(1)} %compare.2.own_mis.source), custom_call_target="tpu_custom_call" | custom-call | flops 6553600 | bytes 524288 | tf_op jit(solution)/shard_map/publish/pallas_call | solution.py:331
  43.4 2.2 %all-gather = f32[4,4,64,128]{3,2,1,0:T(8,128)S(1)} all-gather(f32[2,4,64,128]{3,2,1,0:T(8,128)S(1)} %get-tuple-element.6), channel_id=2, replica_groups={{0,1},{2,3},{4,5},{6,7},{8,9},{10,11},{12,13},{14,15},{16,17},{18,19},{..., dimensions={0}, use_global_device_ids=true | all-gather | bytes 786432 | tf_op jit(solution)/shard_map/all_gather | solution.py:323
  45.6 1.0 %adjoint_chip.1.partial = f32[4,6,80,128]{3,2,1,0:T(8,128)S(1)} custom-call(f32[4,4,64,128]{3,2,1,0:T(8,128)S(1)} %compare.2.own_mis.source, f32[4,4,64,128]{3,2,1,0:T(8,128)S(1)} %pad_maximum_fusion.1.chip_mis), custom_call_target="tpu_custom_call" | custom-call | flops 6553600 | bytes 524288 | tf_op jit(solution)/shard_map/adjoint_chip/pallas_call | solution.py:327
  46.7 5.4 %collective-permute-done.3.prior_ends = f32[4,4,64,128]{3,2,1,0:T(8,128)S(1)} collective-permute-done((f32[4,4,64,128]{3,2,1,0:T(8,128)S(1)}, f32[4,4,64,128]{3,2,1,0:T(8,128)S(1)}, u32[]{:S(2)}, u32[]{:S(2)}) %collective-permute-start.3) | collective-permute-done | bytes 524320 | tf_op jit(solution)/shard_map/ppermute | solution.py:320
  52.1 0.2 carry.1.prior
  52.3 0.0 collective-permute-done.2.cross_mis
  52.3 2.3 %adjoint_cross.1 = f32[4,4,64,128]{3,2,1,0:T(8,128)} custom-call(f32[1]{0:T(128)S(6)} %copy.6.step_size, f32[4,4,64,128]{3,2,1,0:T(8,128)S(1)} %stage.1.own, f32[4,4,64,128]{3,2,1,0:T(8,128)S(1)} %pad_maximum_fusion.chip, f32[4,4,64,128]{3,2,1,0:T(8,128)S(1)} %collective-permute-done.cross, f32[4,4,64,128]{3,2,1,0:T(8,128)S(1)} %compare.2.own_mis.source, ...), custom_call_target="tpu_custom_call" | custom-call | flops 6553600 | bytes 524288 | tf_op jit(solution)/shard_map/adjoint_cross/pallas_call | solution.py:328
  (8 shorter events, 0.2 us)
Async XLA Ops:
  0.6 24.7 %copy-start = (f32[1,4,4,64,128]{4,3,2,1,0:T(8,128)S(1)}, f32[1,4,4,64,128]{4,3,2,1,0:T(8,128)}, u32[]{:S(2)}) copy-start(f32[1,4,4,64,128]{4,3,2,1,0:T(8,128)} %param.3) | copy-start | bytes 1572868
  0.6 27.0 %collective-permute-start = (f32[4,4,64,128]{3,2,1,0:T(8,128)}, f32[4,4,64,128]{3,2,1,0:T(8,128)S(1)}, u32[]{:S(2)}, u32[]{:S(2)}) collective-permute-start(f32[4,4,64,128]{3,2,1,0:T(8,128)} %bitcast.13), channel_id=1, source_target_pairs={{0,31},{1,2},{2,1},{3,4},{4,3},{5,6},{6,5},{7,8},{8,7},{9,10},{10,... | collective-permute-start | bytes 1572872 | tf_op jit(solution)/shard_map/ppermute | solution.py:309
  6.2 23.9 %collective-permute-start.1 = (f32[4,4,64,128]{3,2,1,0:T(8,128)}, f32[4,4,64,128]{3,2,1,0:T(8,128)S(1)}, u32[]{:S(2)}, u32[]{:S(2)}) collective-permute-start(f32[4,4,64,128]{3,2,1,0:T(8,128)} %bitcast.14), channel_id=1, source_target_pairs={{32,0},{64,32},{96,64},{128,96},{160,128},{192,160},{224,192},{256... | collective-permute-start | bytes 1572872 | tf_op jit(solution)/shard_map/ppermute | solution.py:315
  30.1 22.0 %collective-permute-start.3 = (f32[4,4,64,128]{3,2,1,0:T(8,128)S(1)}, f32[4,4,64,128]{3,2,1,0:T(8,128)S(1)}, u32[]{:S(2)}, u32[]{:S(2)}) collective-permute-start(f32[4,4,64,128]{3,2,1,0:T(8,128)S(1)} %forward_chip.1.ends), channel_id=1, source_target_pairs={{0,32},{32,64},{64,96},{96,128},{128,160},{160,192},{192,224},{224... | collective-permute-start | bytes 1572872 | tf_op jit(solution)/shard_map/ppermute | solution.py:320
  32.3 20.0 %collective-permute-start.2 = (f32[4,4,64,128]{3,2,1,0:T(8,128)S(1)}, f32[4,4,64,128]{3,2,1,0:T(8,128)S(1)}, u32[]{:S(2)}, u32[]{:S(2)}) collective-permute-start(f32[4,4,64,128]{3,2,1,0:T(8,128)S(1)} %compare.2.own_mis.source), channel_id=1, source_target_pairs={{0,31},{1,2},{2,1},{3,4},{4,3},{5,6},{6,5},{7,8},{8,7},{9,10},{10,... | collective-permute-start | bytes 1572872 | tf_op jit(solution)/shard_map/ppermute | solution.py:322

commit v4 on v3

--- a/solution.py
+++ b/solution.py
@@ -56,21 +56,36 @@
     return lane_up(f) + lane_down(f) + walls.up(f) + walls.down(f)
 
 
-def explicit(at, put, layers, sign, walls, speed):
+CHUNK = 16
+
+
+def explicit(state, put, layers, sign, speed):
+    rows, columns = speed.shape
+    edges = Walls((CHUNK, columns))
     for layer in layers:
-        here = [at(f, layer) for f in range(4)]
-        d_z = [at(f, layer + 1) - at(f, layer - 1) for f in range(4)]
-        d_th = [lane_up(f) - lane_down(f) for f in here]
-        d_r = [walls.up(f) - walls.down(f) for f in here]
-        u, v, w, p = here
-        by_th = HALF_TAU * (speed + v)
-        by_r = HALF_TAU * u
-        by_z = (HALF_TAU * sign) * w
-        carried = [by_th * d_th[f] + by_r * d_r[f] + by_z * d_z[f] for f in range(3)]
-        put(0, layer, u - (carried[0] + HALF_TAU * d_r[3]) + (2.0 * TAU) * speed * v)
-        put(1, layer, v - (carried[1] + HALF_TAU * d_th[3]) - TAU * speed * u)
-        put(2, layer, w - (carried[2] + (HALF_TAU * sign) * d_z[3]))
-        put(3, layer, p - HALF_TAU * (d_r[0] + d_th[1] + sign * d_z[2]))
+        for row in range(0, rows, CHUNK):
+            b = speed[row : row + CHUNK]
+            u, v, w, p = (state.cut(f, layer, row, CHUNK) for f in range(4))
+            by_th = HALF_TAU * (b + v)
+            by_r = HALF_TAU * u
+            by_z = (HALF_TAU * sign) * w
+
+            def carried(f, here):
+                d_z = state.cut(f, layer + 1, row, CHUNK) - state.cut(f, layer - 1, row, CHUNK)
+                d_th = lane_up(here) - lane_down(here)
+                d_r = state.across(f, layer, row, CHUNK, edges)
+                return d_r, d_th, d_z, by_th * d_th + by_r * d_r + by_z * d_z
+
+            p_r = state.across(3, layer, row, CHUNK, edges)
+            u_r, _, _, moved = carried(0, u)
+            put(0, layer, u - (moved + HALF_TAU * p_r) + (2.0 * TAU) * b * v, row)
+            p_th = lane_up(p) - lane_down(p)
+            _, v_th, _, moved = carried(1, v)
+            put(1, layer, v - (moved + HALF_TAU * p_th) - TAU * b * u, row)
+            p_z = state.cut(3, layer + 1, row, CHUNK) - state.cut(3, layer - 1, row, CHUNK)
+            _, _, w_z, moved = carried(2, w)
+            put(2, layer, w - (moved + (HALF_TAU * sign) * p_z), row)
+            put(3, layer, p - HALF_TAU * (u_r + v_th + sign * w_z), row)
 
 
 PAD = 8
@@ -82,6 +97,18 @@
 
     def get(self, field, layer):
         return layer_of(self.refs, field, layer, self.depth, self.odd)
+
+    def cut(self, field, layer, row, count):
+        behind, own, ahead = self.refs
+        ref = behind if layer < 0 else own if layer < self.depth else ahead
+        return ref[field, place(layer, self.depth, self.odd), row : row + count]
+
+    def across(self, field, layer, row, count, edges):
+        here = self.cut(field, layer, row, count)
+        total = self.refs[1].shape[2]
+        above = self.cut(field, layer, row + 1, count) if row + count < total else edges.up(here)
+        below = self.cut(field, layer, row - 1, count) if row else edges.down(here)
+        return above - below
 
     def up(self, field, layer):
         return self.walls.up(self.get(field, layer))
@@ -95,10 +122,10 @@
         self.parts = parts
         self.rows = parts[0][0].shape[2] - 2 * PAD
 
-    def at(self, field, layer, first):
+    def at(self, field, layer, first, count=None):
         for ref, low, high, start in self.parts:
             if low <= layer < high:
-                return ref[field, start + layer - low, first : first + self.rows]
+                return ref[field, start + layer - low, first : first + (count or self.rows)]
 
     def get(self, field, layer):
         return self.at(field, layer, PAD)
@@ -109,10 +136,10 @@
     def down(self, field, layer):
         return self.at(field, layer, PAD - 1)
 
-    def put(self, field, layer, value):
+    def put(self, field, layer, value, row=0):
         for ref, low, high, start in self.parts:
             if low <= layer < high:
-                ref[field, start + layer - low, PAD : PAD + self.rows] = value
+                ref[field, start + layer - low, PAD + row : PAD + row + value.shape[0]] = value
 
 
 def clear_pads(*refs):
@@ -140,14 +167,13 @@
 def forward_cross_kernel(own, cross, partial, force, first):
     depth, odd, sign, walls, speed = facing(own)
 
-    def at(field, layer):
-        return layer_of((cross, own, None), field, layer, depth, odd)
+    state = Slabs((cross, own, None), depth, odd, walls)
 
     clear_pads(partial, force, first)
     e = Level((force, -3, 0, 0), (partial, 0, depth - 1, 0))
     one = Level((first, -2, 0, 0), (partial, 0, 2, 3))
     two = Level((partial, -1, 1, 5))
-    explicit(at, e.put, range(-3, depth - 1), sign, walls, speed)
+    explicit(state, e.put, range(-3, depth - 1), sign, speed)
     for f in range(4):
         for layer in range(-2, 2):
             one.put(f, layer, (e.get(f, layer) + neighbours(e, f, layer)) * SCALE)
@@ -158,14 +184,13 @@
 def forward_chip_kernel(own, chip, partial, ends, force, first, second):
     depth, odd, sign, walls, speed = facing(own)
 
-    def at(field, layer):
-        return layer_of((None, own, chip), field, layer, depth, odd)
+    state = Slabs((None, own, chip), depth, odd, walls)
 
     clear_pads(force, first, second)
     e = Level((partial, 0, depth - 1, 0), (force, depth - 1, depth + 3, 0))
     one = Level((partial, 0, 2, 3), (first, 2, depth + 2, 0))
     two = Level((partial, -1, 1, 5), (second, 1, depth + 1, 0))
-    explicit(at, e.put, range(depth - 1, depth + 3), sign, walls, speed)
+    explicit(state, e.put, range(depth - 1, depth + 3), sign, speed)
     for f in range(4):
         for layer in range(2, depth + 2):
             one.put(f, layer, (e.get(f, layer) + neighbours(e, f, layer)) * SCALE)
@@ -217,15 +242,24 @@
             total.put(f, layer, (c.get(f, layer) + one.get(f, layer) + two.get(f, layer) + last) * SCALE)
 
 
-def adjoint_cross_kernel(step_size, own, chip, cross, own_mis, cross_mis, prior, partial, updated, cot, first, second):
+def slopes_kernel(own, chip, cross, slopes):
     depth, odd, sign, walls, speed = facing(own, 1)
-
-    def at(field, layer):
-        return layer_of((chip, own, cross), field, layer, depth, odd)
-
+    state = Slabs((chip, own, cross), depth, odd, walls)
+    for layer in range(depth):
+        for f in range(3):
+            here = state.get(f, layer)
+            slopes[f, layer] = lane_up(here) - lane_down(here)
+            slopes[3 + f, layer] = walls.up(here) - walls.down(here)
+            slopes[6 + f, layer] = state.get(f, layer + 1) - state.get(f, layer - 1)
+
+
+def adjoint_cross_kernel(step_size, own, chip, cross, own_mis, cross_mis, prior, slopes, partial, updated, cot, first, second, flux):
+    depth, odd, sign, walls, speed = facing(own, 1)
+
+    state = Slabs((chip, own, cross), depth, odd, walls)
     c = Slabs((None, own_mis, cross_mis), depth, odd, walls)
 
-    clear_pads(cot, first, second)
+    clear_pads(cot, first, second, flux)
     one = Level((partial, 1, 3, 2), (first, 3, depth + 3, 0))
     two = Level((partial, 0, 2, 4), (second, 2, depth + 2, 0))
     total = Level((partial, -1, 1, 0), (cot, 1, depth + 1, 0))
@@ -240,36 +274,48 @@
 
     size = step_size[0]
     half = HALF_TAU
+    moving = Level((flux, 0, depth, 0))
+    for layer in range(depth):
+        u = state.get(0, layer)
+        moving.put(0, layer, u * total.get(0, layer) + total.get(3, layer))
+        moving.put(1, layer, u * total.get(1, layer))
+        moving.put(2, layer, u * total.get(2, layer))
 
     def th(f):
         return lane_up(f) - lane_down(f)
 
-    def rad(f):
-        return walls.up(f) - walls.down(f)
-
     for layer in range(depth):
-        here = [at(f, layer) for f in range(4)]
-        u, v, w, p = here
-        c0, c1, c2, c3 = (total.get(f, layer) for f in range(4))
-        below = [total.get(f, layer - 1) for f in range(4)]
-        above = [total.get(f, layer + 1) for f in range(4)]
-        w_below, w_above = at(2, layer - 1), at(2, layer + 1)
-        swirl = speed + v
-        pull_r = c0 * rad(u) + c1 * rad(v) + c2 * rad(w)
-        pull_th = c0 * th(u) + c1 * th(v) + c2 * th(w)
-        pull_z = sum(x * (at(f, layer + 1) - at(f, layer - 1)) for f, x in ((0, c0), (1, c1), (2, c2)))
-        axial = [w_above * above[f] - w_below * below[f] for f in range(3)]
-        grads = [
-            c0 + half * (th(swirl * c0) + rad(u * c0 + c3) + sign * axial[0] - pull_r) - TAU * speed * c1,
-            c1
-            + half * (th(swirl * c1 + c3) + rad(u * c1) + sign * axial[1] - pull_th)
-            + (2.0 * TAU) * speed * c0,
-            c2 + half * (th(swirl * c2) + rad(u * c2) + sign * (axial[2] + above[3] - below[3] - pull_z)),
-            c3 + half * (total.up(0, layer) - total.down(0, layer) + th(c1) + sign * (above[2] - below[2])),
-        ]
         to = place(layer, depth, odd)
-        for f in range(4):
-            updated[f, to] = here[f] - size * (grads[f] - prior[f, to])
+        for row in range(0, own.shape[2], CHUNK):
+            at = PAD + row
+
+            def rad(level, f):
+                return level.at(f, layer, at + 1, CHUNK) - level.at(f, layer, at - 1, CHUNK)
+
+            def slope(f):
+                return slopes[f, layer, row : row + CHUNK]
+
+            def write(f, here, grad):
+                updated[f, to, row : row + CHUNK] = here - size * (grad - prior[f, to, row : row + CHUNK])
+
+            u, v, w, p = (state.cut(f, layer, row, CHUNK) for f in range(4))
+            b = speed[row : row + CHUNK]
+            c0, c1, c2, c3 = (total.at(f, layer, at, CHUNK) for f in range(4))
+            below = [total.at(f, layer - 1, at, CHUNK) for f in range(4)]
+            above = [total.at(f, layer + 1, at, CHUNK) for f in range(4)]
+            w_below, w_above = state.cut(2, layer - 1, row, CHUNK), state.cut(2, layer + 1, row, CHUNK)
+            swirl = b + v
+            axial = [w_above * above[f] - w_below * below[f] for f in range(3)]
+            pull = c0 * slope(3) + c1 * slope(4) + c2 * slope(5)
+            step = half * (th(swirl * c0) + rad(moving, 0) + sign * axial[0] - pull)
+            write(0, u, c0 + step - TAU * b * c1)
+            pull = c0 * slope(0) + c1 * slope(1) + c2 * slope(2)
+            step = half * (th(swirl * c1 + c3) + rad(moving, 1) + sign * axial[1] - pull)
+            write(1, v, c1 + step + (2.0 * TAU) * b * c0)
+            pull = c0 * slope(6) + c1 * slope(7) + c2 * slope(8)
+            step = half * (th(swirl * c2) + rad(moving, 2) + sign * (axial[2] + above[3] - below[3] - pull))
+            write(2, w, c2 + step)
+            write(3, p, c3 + half * (rad(total, 0) + th(c1) + sign * (above[2] - below[2])))
 
 
 def copy_kernel(source, own):
@@ -283,15 +329,15 @@
 SMEM = pl.BlockSpec(memory_space=pltpu.SMEM)
 
 
-def kernel(body, like, ins, out_layers, scratch_layers=(), name=None, passes=50, pad=0):
-    fields, depth, rows, columns = like.shape
+def kernel(body, like, ins, out_layers, scratch_layers=(), name=None, passes=50, pad=0, fields=4):
+    _, depth, rows, columns = like.shape
     size = fields * depth * rows * columns
     return pl.pallas_call(
         body,
         out_shape=jax.ShapeDtypeStruct((fields, out_layers, rows + 2 * pad, columns), jnp.float32),
         in_specs=ins,
         out_specs=VMEM,
-        scratch_shapes=[pltpu.VMEM((fields, n, rows + 2 * PAD, columns), jnp.float32) for n in scratch_layers],
+        scratch_shapes=[pltpu.VMEM((4, n, rows + 2 * PAD, columns), jnp.float32) for n in scratch_layers],
         cost_estimate=pl.CostEstimate(flops=passes * size, bytes_accessed=4 * size, transcendentals=0),
         compiler_params=PARAMS,
         name=name,
@@ -325,8 +371,9 @@
     chip_mis = jnp.concatenate([low[other], high[other]])
     prior = kernel(carry_kernel, start, [SMEM, VMEM, VMEM], depth, (), "carry", 2)(shift, own, prior_ends)
     partial = kernel(adjoint_chip_kernel, start, [VMEM] * 2, 6, (4, 2), "adjoint_chip", pad=PAD)(mismatch, chip_mis)
-    updated = kernel(adjoint_cross_kernel, start, [SMEM] + [VMEM] * 7, depth, (4, 4, 4), "adjoint_cross")(
-        step_size, own, chip, cross, mismatch, cross_mis, prior, partial
+    slopes = kernel(slopes_kernel, start, [VMEM] * 3, depth, (), "slopes", fields=9)(own, chip, cross)
+    updated = kernel(adjoint_cross_kernel, start, [SMEM] + [VMEM] * 8, depth, (4, 4, 4, depth), "adjoint_cross")(
+        step_size, own, chip, cross, mismatch, cross_mis, prior, slopes, partial
     )
     shown = kernel(copy_kernel, start, [VMEM], depth, name="publish")(mismatch)
     return updated[None], shown[None]

time: 54.9 us -> 54 us (0.984)
  waiting for transfers between devices: 5.39 us -> 4.45 us
    ppermute x1, waiting for transfers between devices: 5.38 us -> 4.44 us  [per_device(): prior_ends = lax.ppermute(ends, 'tm', forth)]
    pallas_call x1 -> x2, Pallas kernels: 2.28 us -> 2.35 us  [the longest x1 2.07 us: per_device(): kernel(adjoint_cross_kernel, start, [SMEM] + [VMEM] * 8, depth, (4, 4, 4,...]
where the time goes in v4:
time: 54 us; the launch traced here: 53.7 us
  blocking collectives  22.1 us (41%)
  starting transfers between devices  16.9 us (31%)
  Pallas kernels  6.86 us (13%)
  waiting for transfers between devices  4.45 us (8%)
  between operations  2.1 us (4%)
  local copies, waits for them, and re-layouts  1.19 us (2%)
    all_gather x1, blocking collectives, per_device(): high = lax.all_gather(start[2:], 'gz', axis_index_groups=pairs)  9.22 us
    all_gather x1, blocking collectives, per_device(): high = lax.all_gather(mismatch[2:], 'gz', axis_index_groups=pairs)  8.52 us
    ppermute x1, starting transfers between devices, per_device(): following = lax.ppermute(start, 'tm', back)  7.56 us
    ppermute x1, starting transfers between devices, per_device(): cross = lax.ppermute(start, 'gz', next_chip)  5.52 us
    ppermute x1, waiting for transfers between devices, per_device(): prior_ends = lax.ppermute(ends, 'tm', forth)  4.44 us
    all_gather x1, blocking collectives, per_device(): low = lax.all_gather(start[:2], 'gz', axis_index_groups=pairs)  2.18 us
    all_gather x1, blocking collectives, per_device(): low = lax.all_gather(mismatch[:2], 'gz', axis_index_groups=pairs)  2.18 us
    pallas_call x1, Pallas kernels, per_device(): kernel(adjoint_cross_kernel, start, [SMEM] + [VMEM] * 8, depth, (4, 4, 4,...  2.07 us
  transfers between devices with their start and end apart: 4, of which 1 were waited for; matrix products, arithmetic and copies ran while one was open for 2% of the time, Pallas kernels for 9%

profile of v4, /device:TPU:1, one launch (start us, length us, event | category | flops | bytes accessed | tf_op | source)
XLA Modules:
  0.0 53.7 jit_solution(7723185919828275764)
XLA Ops:
  0.6 0.0 copy-start
  0.6 5.5 %collective-permute-start = (f32[4,4,64,128]{3,2,1,0:T(8,128)}, f32[4,4,64,128]{3,2,1,0:T(8,128)S(1)}, u32[]{:S(2)}, u32[]{:S(2)}) collective-permute-start(f32[4,4,64,128]{3,2,1,0:T(8,128)} %bitcast.13), channel_id=1, source_target_pairs={{0,31},{1,2},{2,1},{3,4},{4,3},{5,6},{6,5},{7,8},{8,7},{9,10},{10,... | collective-permute-start | bytes 1572872 | tf_op jit(solution)/shard_map/ppermute | solution.py:355
  6.2 7.6 %collective-permute-start.1 = (f32[4,4,64,128]{3,2,1,0:T(8,128)}, f32[4,4,64,128]{3,2,1,0:T(8,128)S(1)}, u32[]{:S(2)}, u32[]{:S(2)}) collective-permute-start(f32[4,4,64,128]{3,2,1,0:T(8,128)} %bitcast.14), channel_id=1, source_target_pairs={{32,0},{64,32},{96,64},{128,96},{160,128},{192,160},{224,192},{256... | collective-permute-start | bytes 1572872 | tf_op jit(solution)/shard_map/ppermute | solution.py:361
  13.7 1.1 %fusion.1 = (f32[1,2,4,64,128]{4,3,2,1,0:T(8,128)S(1)}, f32[1,2,4,64,128]{4,3,2,1,0:T(8,128)S(1)}) fusion(f32[1,4,4,64,128]{4,3,2,1,0:T(8,128)} %param.3), kind=kLoop, calls=%fused_computation.7 | loop fusion | bytes 1048576 | tf_op jit(solution)/shard_map/slice | solution.py:358
  14.8 9.2 %all_gather.21 = f32[2,2,4,64,128]{4,3,2,1,0:T(8,128)S(1)} all-gather(f32[1,2,4,64,128]{4,3,2,1,0:T(8,128)S(1)} %get-tuple-element.9), channel_id=1, replica_groups={{0,1},{2,3},{4,5},{6,7},{8,9},{10,11},{12,13},{14,15},{16,17},{18,19},{..., dimensions={0}, use_global_device_ids=true | all-gather | bytes 786432 | tf_op jit(solution)/shard_map/all_gather | solution.py:359
  25.3 0.0 copy-done
  25.4 2.2 %all_gather.20 = f32[2,2,4,64,128]{4,3,2,1,0:T(8,128)S(1)} all-gather(f32[1,2,4,64,128]{4,3,2,1,0:T(8,128)S(1)} %get-tuple-element.8), channel_id=1, replica_groups={{0,1},{2,3},{4,5},{6,7},{8,9},{10,11},{12,13},{14,15},{16,17},{18,19},{..., dimensions={0}, use_global_device_ids=true | all-gather | bytes 786432 | tf_op jit(solution)/shard_map/all_gather | solution.py:358
  27.7 0.0 collective-permute-done.cross
  27.7 1.0 %forward_cross.1.partial = f32[4,7,80,128]{3,2,1,0:T(8,128)S(1)} custom-call(f32[4,4,64,128]{3,2,1,0:T(8,128)S(1)} %stage.1.own, f32[4,4,64,128]{3,2,1,0:T(8,128)S(1)} %collective-permute-done.cross), custom_call_target="tpu_custom_call" | custom-call | flops 6553600 | bytes 524288 | tf_op jit(solution)/shard_map/forward_cross/pallas_call | solution.py:363
  28.7 1.2 %forward_chip.1.ends = f32[4,4,64,128]{3,2,1,0:T(8,128)S(1)} custom-call(f32[4,4,64,128]{3,2,1,0:T(8,128)S(1)} %stage.1.own, f32[4,4,64,128]{3,2,1,0:T(8,128)S(1)} %pad_maximum_fusion.chip, f32[4,7,80,128]{3,2,1,0:T(8,128)S(1)} %forward_cross.1.partial), custom_call_target="tpu_custom_call" | custom-call | flops 6553600 | bytes 524288 | tf_op jit(solution)/shard_map/forward_chip/pallas_call | solution.py:364
  29.9 0.0 collective-permute-done.1.following
  29.9 1.9 %collective-permute-start.3 = (f32[4,4,64,128]{3,2,1,0:T(8,128)S(1)}, f32[4,4,64,128]{3,2,1,0:T(8,128)S(1)}, u32[]{:S(2)}, u32[]{:S(2)}) collective-permute-start(f32[4,4,64,128]{3,2,1,0:T(8,128)S(1)} %forward_chip.1.ends), channel_id=1, source_target_pairs={{0,32},{32,64},{64,96},{96,128},{128,160},{160,192},{192,224},{224... | collective-permute-start | bytes 1572872 | tf_op jit(solution)/shard_map/ppermute | solution.py:366
  31.8 0.2 compare.2.own_mis.source
  32.1 1.9 %collective-permute-start.2 = (f32[4,4,64,128]{3,2,1,0:T(8,128)S(1)}, f32[4,4,64,128]{3,2,1,0:T(8,128)S(1)}, u32[]{:S(2)}, u32[]{:S(2)}) collective-permute-start(f32[4,4,64,128]{3,2,1,0:T(8,128)S(1)} %compare.2.own_mis.source), channel_id=1, source_target_pairs={{0,31},{1,2},{2,1},{3,4},{4,3},{5,6},{6,5},{7,8},{8,7},{9,10},{10,... | collective-permute-start | bytes 1572872 | tf_op jit(solution)/shard_map/ppermute | solution.py:368
  34.0 8.5 %all-gather.1 = f32[4,4,64,128]{3,2,1,0:T(8,128)S(1)} all-gather(f32[2,4,64,128]{3,2,1,0:T(8,128)S(1)} %get-tuple-element.7), channel_id=3, replica_groups={{0,1},{2,3},{4,5},{6,7},{8,9},{10,11},{12,13},{14,15},{16,17},{18,19},{..., dimensions={0}, use_global_device_ids=true | all-gather | bytes 786432 | tf_op jit(solution)/shard_map/all_gather | solution.py:370
  42.5 0.8 %publish.1 = f32[4,4,64,128]{3,2,1,0:T(8,128)} custom-call(f32[4,4,64,128]{3,2,1,0:T(8,128)S(1)} %compare.2.own_mis.source), custom_call_target="tpu_custom_call" | custom-call | flops 6553600 | bytes 524288 | tf_op jit(solution)/shard_map/publish/pallas_call | solution.py:378
  43.4 2.2 %all-gather = f32[4,4,64,128]{3,2,1,0:T(8,128)S(1)} all-gather(f32[2,4,64,128]{3,2,1,0:T(8,128)S(1)} %get-tuple-element.6), channel_id=2, replica_groups={{0,1},{2,3},{4,5},{6,7},{8,9},{10,11},{12,13},{14,15},{16,17},{18,19},{..., dimensions={0}, use_global_device_ids=true | all-gather | bytes 786432 | tf_op jit(solution)/shard_map/all_gather | solution.py:369
  45.6 1.0 %adjoint_chip.1.partial = f32[4,6,80,128]{3,2,1,0:T(8,128)S(1)} custom-call(f32[4,4,64,128]{3,2,1,0:T(8,128)S(1)} %compare.2.own_mis.source, f32[4,4,64,128]{3,2,1,0:T(8,128)S(1)} %pad_maximum_fusion.1.chip_mis), custom_call_target="tpu_custom_call" | custom-call | flops 6553600 | bytes 524288 | tf_op jit(solution)/shard_map/adjoint_chip/pallas_call | solution.py:373
  46.7 0.3 slopes.1
  47.0 4.4 %collective-permute-done.3.prior_ends = f32[4,4,64,128]{3,2,1,0:T(8,128)S(1)} collective-permute-done((f32[4,4,64,128]{3,2,1,0:T(8,128)S(1)}, f32[4,4,64,128]{3,2,1,0:T(8,128)S(1)}, u32[]{:S(2)}, u32[]{:S(2)}) %collective-permute-start.3) | collective-permute-done | bytes 524320 | tf_op jit(solution)/shard_map/ppermute | solution.py:366
  51.4 0.2 carry.1.prior
  51.6 0.0 collective-permute-done.2.cross_mis
  51.6 2.1 %adjoint_cross.1 = f32[4,4,64,128]{3,2,1,0:T(8,128)} custom-call(f32[1]{0:T(128)S(6)} %copy.6.step_size, f32[4,4,64,128]{3,2,1,0:T(8,128)S(1)} %stage.1.own, f32[4,4,64,128]{3,2,1,0:T(8,128)S(1)} %pad_maximum_fusion.chip, f32[4,4,64,128]{3,2,1,0:T(8,128)S(1)} %collective-permute-done.cross, f32[4,4,64,128]{3,2,1,0:T(8,128)S(1)} %compare.2.own_mis.source, ...), custom_call_target="tpu_custom_call" | custom-call | flops 6553600 | bytes 524288 | tf_op jit(solution)/shard_map/adjoint_cross/pallas_call | solution.py:375
  (8 shorter events, 0.2 us)
Async XLA Ops:
  0.6 24.7 %copy-start = (f32[1,4,4,64,128]{4,3,2,1,0:T(8,128)S(1)}, f32[1,4,4,64,128]{4,3,2,1,0:T(8,128)}, u32[]{:S(2)}) copy-start(f32[1,4,4,64,128]{4,3,2,1,0:T(8,128)} %param.3) | copy-start | bytes 1572868
  0.6 27.0 %collective-permute-start = (f32[4,4,64,128]{3,2,1,0:T(8,128)}, f32[4,4,64,128]{3,2,1,0:T(8,128)S(1)}, u32[]{:S(2)}, u32[]{:S(2)}) collective-permute-start(f32[4,4,64,128]{3,2,1,0:T(8,128)} %bitcast.13), channel_id=1, source_target_pairs={{0,31},{1,2},{2,1},{3,4},{4,3},{5,6},{6,5},{7,8},{8,7},{9,10},{10,... | collective-permute-start | bytes 1572872 | tf_op jit(solution)/shard_map/ppermute | solution.py:355
  6.2 23.7 %collective-permute-start.1 = (f32[4,4,64,128]{3,2,1,0:T(8,128)}, f32[4,4,64,128]{3,2,1,0:T(8,128)S(1)}, u32[]{:S(2)}, u32[]{:S(2)}) collective-permute-start(f32[4,4,64,128]{3,2,1,0:T(8,128)} %bitcast.14), channel_id=1, source_target_pairs={{32,0},{64,32},{96,64},{128,96},{160,128},{192,160},{224,192},{256... | collective-permute-start | bytes 1572872 | tf_op jit(solution)/shard_map/ppermute | solution.py:361
  29.9 21.5 %collective-permute-start.3 = (f32[4,4,64,128]{3,2,1,0:T(8,128)S(1)}, f32[4,4,64,128]{3,2,1,0:T(8,128)S(1)}, u32[]{:S(2)}, u32[]{:S(2)}) collective-permute-start(f32[4,4,64,128]{3,2,1,0:T(8,128)S(1)} %forward_chip.1.ends), channel_id=1, source_target_pairs={{0,32},{32,64},{64,96},{96,128},{128,160},{160,192},{192,224},{224... | collective-permute-start | bytes 1572872 | tf_op jit(solution)/shard_map/ppermute | solution.py:366
  32.1 19.5 %collective-permute-start.2 = (f32[4,4,64,128]{3,2,1,0:T(8,128)S(1)}, f32[4,4,64,128]{3,2,1,0:T(8,128)S(1)}, u32[]{:S(2)}, u32[]{:S(2)}) collective-permute-start(f32[4,4,64,128]{3,2,1,0:T(8,128)S(1)} %compare.2.own_mis.source), channel_id=1, source_target_pairs={{0,31},{1,2},{2,1},{3,4},{4,3},{5,6},{6,5},{7,8},{8,7},{9,10},{10,... | collective-permute-start | bytes 1572872 | tf_op jit(solution)/shard_map/ppermute | solution.py:368

commit v5 on v4

--- a/solution.py
+++ b/solution.py
@@ -56,7 +56,7 @@
     return lane_up(f) + lane_down(f) + walls.up(f) + walls.down(f)
 
 
-CHUNK = 16
+CHUNK = 8
 
 
 def explicit(state, put, layers, sign, speed):
@@ -253,7 +253,7 @@
             slopes[6 + f, layer] = state.get(f, layer + 1) - state.get(f, layer - 1)
 
 
-def adjoint_cross_kernel(step_size, own, chip, cross, own_mis, cross_mis, prior, slopes, partial, updated, cot, first, second, flux):
+def adjoint_cross_kernel(step_size, own, chip, cross, own_mis, cross_mis, prior, slopes, partial, updated, cot, first, second, flux, done, sems):
     depth, odd, sign, walls, speed = facing(own, 1)
 
     state = Slabs((chip, own, cross), depth, odd, walls)
@@ -263,19 +263,16 @@
     one = Level((partial, 1, 3, 2), (first, 3, depth + 3, 0))
     two = Level((partial, 0, 2, 4), (second, 2, depth + 2, 0))
     total = Level((partial, -1, 1, 0), (cot, 1, depth + 1, 0))
-    for f in range(4):
-        for layer in range(3, depth + 3):
-            one.put(f, layer, neighbours(c, f, layer) * SCALE)
-        for layer in range(2, depth + 2):
-            two.put(f, layer, neighbours(one, f, layer) * SCALE)
-        for layer in range(1, depth + 1):
-            last = neighbours(two, f, layer)
-            total.put(f, layer, (c.get(f, layer) + one.get(f, layer) + two.get(f, layer) + last) * SCALE)
-
     size = step_size[0]
     half = HALF_TAU
     moving = Level((flux, 0, depth, 0))
-    for layer in range(depth):
+    def advance(layer):
+        for f in range(4):
+            one.put(f, layer + 3, neighbours(c, f, layer + 3) * SCALE)
+            two.put(f, layer + 2, neighbours(one, f, layer + 2) * SCALE)
+            near = layer + 1
+            last = neighbours(two, f, near)
+            total.put(f, near, (c.get(f, near) + one.get(f, near) + two.get(f, near) + last) * SCALE)
         u = state.get(0, layer)
         moving.put(0, layer, u * total.get(0, layer) + total.get(3, layer))
         moving.put(1, layer, u * total.get(1, layer))
@@ -284,7 +281,9 @@
     def th(f):
         return lane_up(f) - lane_down(f)
 
+    copies = []
     for layer in range(depth):
+        advance(layer)
         to = place(layer, depth, odd)
         for row in range(0, own.shape[2], CHUNK):
             at = PAD + row
@@ -296,7 +295,7 @@
                 return slopes[f, layer, row : row + CHUNK]
 
             def write(f, here, grad):
-                updated[f, to, row : row + CHUNK] = here - size * (grad - prior[f, to, row : row + CHUNK])
+                done[f, layer, row : row + CHUNK] = here - size * (grad - prior[f, to, row : row + CHUNK])
 
             u, v, w, p = (state.cut(f, layer, row, CHUNK) for f in range(4))
             b = speed[row : row + CHUNK]
@@ -316,6 +315,12 @@
             step = half * (th(swirl * c2) + rad(moving, 2) + sign * (axial[2] + above[3] - below[3] - pull))
             write(2, w, c2 + step)
             write(3, p, c3 + half * (rad(total, 0) + th(c1) + sign * (above[2] - below[2])))
+        for f in range(4):
+            source = done.at[f, layer, pl.ds(0, own.shape[2])]
+            copies.append(pltpu.make_async_copy(source, updated.at[f, to], sems.at[f, layer]))
+            copies[-1].start()
+    for copy in copies:
+        copy.wait()
 
 
 def copy_kernel(source, own):
@@ -326,18 +331,19 @@
 
 VMEM = pl.BlockSpec(memory_space=pltpu.VMEM)
 PARAMS = pltpu.CompilerParams(vmem_limit_bytes=16 * 2**20)
+HBM = pl.BlockSpec(memory_space=pltpu.HBM)
 SMEM = pl.BlockSpec(memory_space=pltpu.SMEM)
 
 
-def kernel(body, like, ins, out_layers, scratch_layers=(), name=None, passes=50, pad=0, fields=4):
+def kernel(body, like, ins, out_layers, scratch_layers=(), name=None, passes=50, pad=0, fields=4, out=VMEM, extra=()):
     _, depth, rows, columns = like.shape
     size = fields * depth * rows * columns
     return pl.pallas_call(
         body,
         out_shape=jax.ShapeDtypeStruct((fields, out_layers, rows + 2 * pad, columns), jnp.float32),
         in_specs=ins,
-        out_specs=VMEM,
-        scratch_shapes=[pltpu.VMEM((4, n, rows + 2 * PAD, columns), jnp.float32) for n in scratch_layers],
+        out_specs=out,
+        scratch_shapes=[pltpu.VMEM((4, n, rows + 2 * PAD, columns), jnp.float32) for n in scratch_layers] + list(extra),
         cost_estimate=pl.CostEstimate(flops=passes * size, bytes_accessed=4 * size, transcendentals=0),
         compiler_params=PARAMS,
         name=name,
@@ -372,7 +378,8 @@
     prior = kernel(carry_kernel, start, [SMEM, VMEM, VMEM], depth, (), "carry", 2)(shift, own, prior_ends)
     partial = kernel(adjoint_chip_kernel, start, [VMEM] * 2, 6, (4, 2), "adjoint_chip", pad=PAD)(mismatch, chip_mis)
     slopes = kernel(slopes_kernel, start, [VMEM] * 3, depth, (), "slopes", fields=9)(own, chip, cross)
-    updated = kernel(adjoint_cross_kernel, start, [SMEM] + [VMEM] * 8, depth, (4, 4, 4, depth), "adjoint_cross")(
+    sems = pltpu.SemaphoreType.DMA((4, depth))
+    updated = kernel(adjoint_cross_kernel, start, [SMEM] + [VMEM] * 8, depth, (4, 4, 4, depth, depth), "adjoint_cross", out=HBM, extra=[sems])(
         step_size, own, chip, cross, mismatch, cross_mis, prior, slopes, partial
     )
     shown = kernel(copy_kernel, start, [VMEM], depth, name="publish")(mismatch)

time: 54 us -> 53.9 us (level)
  no operation moved by 1% of the time
where the time goes in v5:
time: 53.9 us; the launch traced here: 53.6 us
  blocking collectives  22.1 us (41%)
  starting transfers between devices  16.9 us (31%)
  Pallas kernels  6.79 us (13%)
  waiting for transfers between devices  4.45 us (8%)
  between operations  2.1 us (4%)
  local copies, waits for them, and re-layouts  1.19 us (2%)
    all_gather x1, blocking collectives, per_device(): high = lax.all_gather(start[2:], 'gz', axis_index_groups=pairs)  9.22 us
    all_gather x1, blocking collectives, per_device(): high = lax.all_gather(mismatch[2:], 'gz', axis_index_groups=pairs)  8.52 us
    ppermute x1, starting transfers between devices, per_device(): following = lax.ppermute(start, 'tm', back)  7.56 us
    ppermute x1, starting transfers between devices, per_device(): cross = lax.ppermute(start, 'gz', next_chip)  5.52 us
    ppermute x1, waiting for transfers between devices, per_device(): prior_ends = lax.ppermute(ends, 'tm', forth)  4.44 us
    all_gather x1, blocking collectives, per_device(): low = lax.all_gather(start[:2], 'gz', axis_index_groups=pairs)  2.18 us
    all_gather x1, blocking collectives, per_device(): low = lax.all_gather(mismatch[:2], 'gz', axis_index_groups=pairs)  2.18 us
    pallas_call x1, Pallas kernels, per_device(): kernel(adjoint_cross_kernel, start, [SMEM] + [VMEM] * 8, depth, (4, 4, 4,...  2 us
  transfers between devices with their start and end apart: 4, of which 1 were waited for; matrix products, arithmetic and copies ran while one was open for 2% of the time, Pallas kernels for 9%

profile of v5, /device:TPU:1, one launch (start us, length us, event | category | flops | bytes accessed | tf_op | source)
XLA Modules:
  0.0 53.6 jit_solution(17217097869987799491)
XLA Ops:
  0.6 0.0 copy-start
  0.6 5.5 %collective-permute-start = (f32[4,4,64,128]{3,2,1,0:T(8,128)}, f32[4,4,64,128]{3,2,1,0:T(8,128)S(1)}, u32[]{:S(2)}, u32[]{:S(2)}) collective-permute-start(f32[4,4,64,128]{3,2,1,0:T(8,128)} %bitcast.13), channel_id=1, source_target_pairs={{0,31},{1,2},{2,1},{3,4},{4,3},{5,6},{6,5},{7,8},{8,7},{9,10},{10,... | collective-permute-start | bytes 1572872 | tf_op jit(solution)/shard_map/ppermute | solution.py:361
  6.2 7.6 %collective-permute-start.1 = (f32[4,4,64,128]{3,2,1,0:T(8,128)}, f32[4,4,64,128]{3,2,1,0:T(8,128)S(1)}, u32[]{:S(2)}, u32[]{:S(2)}) collective-permute-start(f32[4,4,64,128]{3,2,1,0:T(8,128)} %bitcast.14), channel_id=1, source_target_pairs={{32,0},{64,32},{96,64},{128,96},{160,128},{192,160},{224,192},{256... | collective-permute-start | bytes 1572872 | tf_op jit(solution)/shard_map/ppermute | solution.py:367
  13.7 1.1 %fusion.1 = (f32[1,2,4,64,128]{4,3,2,1,0:T(8,128)S(1)}, f32[1,2,4,64,128]{4,3,2,1,0:T(8,128)S(1)}) fusion(f32[1,4,4,64,128]{4,3,2,1,0:T(8,128)} %param.3), kind=kLoop, calls=%fused_computation.7 | loop fusion | bytes 1048576 | tf_op jit(solution)/shard_map/slice | solution.py:364
  14.8 9.2 %all_gather.21 = f32[2,2,4,64,128]{4,3,2,1,0:T(8,128)S(1)} all-gather(f32[1,2,4,64,128]{4,3,2,1,0:T(8,128)S(1)} %get-tuple-element.9), channel_id=1, replica_groups={{0,1},{2,3},{4,5},{6,7},{8,9},{10,11},{12,13},{14,15},{16,17},{18,19},{..., dimensions={0}, use_global_device_ids=true | all-gather | bytes 786432 | tf_op jit(solution)/shard_map/all_gather | solution.py:365
  25.3 0.0 copy-done
  25.4 2.2 %all_gather.20 = f32[2,2,4,64,128]{4,3,2,1,0:T(8,128)S(1)} all-gather(f32[1,2,4,64,128]{4,3,2,1,0:T(8,128)S(1)} %get-tuple-element.8), channel_id=1, replica_groups={{0,1},{2,3},{4,5},{6,7},{8,9},{10,11},{12,13},{14,15},{16,17},{18,19},{..., dimensions={0}, use_global_device_ids=true | all-gather | bytes 786432 | tf_op jit(solution)/shard_map/all_gather | solution.py:364
  27.7 0.0 collective-permute-done.cross
  27.7 1.0 %forward_cross.1.partial = f32[4,7,80,128]{3,2,1,0:T(8,128)S(1)} custom-call(f32[4,4,64,128]{3,2,1,0:T(8,128)S(1)} %stage.1.own, f32[4,4,64,128]{3,2,1,0:T(8,128)S(1)} %collective-permute-done.cross), custom_call_target="tpu_custom_call" | custom-call | flops 6553600 | bytes 524288 | tf_op jit(solution)/shard_map/forward_cross/pallas_call | solution.py:369
  28.7 1.2 %forward_chip.1.ends = f32[4,4,64,128]{3,2,1,0:T(8,128)S(1)} custom-call(f32[4,4,64,128]{3,2,1,0:T(8,128)S(1)} %stage.1.own, f32[4,4,64,128]{3,2,1,0:T(8,128)S(1)} %pad_maximum_fusion.chip, f32[4,7,80,128]{3,2,1,0:T(8,128)S(1)} %forward_cross.1.partial), custom_call_target="tpu_custom_call" | custom-call | flops 6553600 | bytes 524288 | tf_op jit(solution)/shard_map/forward_chip/pallas_call | solution.py:370
  29.9 0.0 collective-permute-done.1.following
  29.9 1.9 %collective-permute-start.3 = (f32[4,4,64,128]{3,2,1,0:T(8,128)S(1)}, f32[4,4,64,128]{3,2,1,0:T(8,128)S(1)}, u32[]{:S(2)}, u32[]{:S(2)}) collective-permute-start(f32[4,4,64,128]{3,2,1,0:T(8,128)S(1)} %forward_chip.1.ends), channel_id=1, source_target_pairs={{0,32},{32,64},{64,96},{96,128},{128,160},{160,192},{192,224},{224... | collective-permute-start | bytes 1572872 | tf_op jit(solution)/shard_map/ppermute | solution.py:372
  31.8 0.2 compare.2.own_mis.source
  32.1 1.9 %collective-permute-start.2 = (f32[4,4,64,128]{3,2,1,0:T(8,128)S(1)}, f32[4,4,64,128]{3,2,1,0:T(8,128)S(1)}, u32[]{:S(2)}, u32[]{:S(2)}) collective-permute-start(f32[4,4,64,128]{3,2,1,0:T(8,128)S(1)} %compare.2.own_mis.source), channel_id=1, source_target_pairs={{0,31},{1,2},{2,1},{3,4},{4,3},{5,6},{6,5},{7,8},{8,7},{9,10},{10,... | collective-permute-start | bytes 1572872 | tf_op jit(solution)/shard_map/ppermute | solution.py:374
  34.0 8.5 %all-gather.1 = f32[4,4,64,128]{3,2,1,0:T(8,128)S(1)} all-gather(f32[2,4,64,128]{3,2,1,0:T(8,128)S(1)} %get-tuple-element.7), channel_id=3, replica_groups={{0,1},{2,3},{4,5},{6,7},{8,9},{10,11},{12,13},{14,15},{16,17},{18,19},{..., dimensions={0}, use_global_device_ids=true | all-gather | bytes 786432 | tf_op jit(solution)/shard_map/all_gather | solution.py:376
  42.5 0.8 %publish.1 = f32[4,4,64,128]{3,2,1,0:T(8,128)} custom-call(f32[4,4,64,128]{3,2,1,0:T(8,128)S(1)} %compare.2.own_mis.source), custom_call_target="tpu_custom_call" | custom-call | flops 6553600 | bytes 524288 | tf_op jit(solution)/shard_map/publish/pallas_call | solution.py:385
  43.4 2.2 %all-gather = f32[4,4,64,128]{3,2,1,0:T(8,128)S(1)} all-gather(f32[2,4,64,128]{3,2,1,0:T(8,128)S(1)} %get-tuple-element.6), channel_id=2, replica_groups={{0,1},{2,3},{4,5},{6,7},{8,9},{10,11},{12,13},{14,15},{16,17},{18,19},{..., dimensions={0}, use_global_device_ids=true | all-gather | bytes 786432 | tf_op jit(solution)/shard_map/all_gather | solution.py:375
  45.6 1.0 %adjoint_chip.1.partial = f32[4,6,80,128]{3,2,1,0:T(8,128)S(1)} custom-call(f32[4,4,64,128]{3,2,1,0:T(8,128)S(1)} %compare.2.own_mis.source, f32[4,4,64,128]{3,2,1,0:T(8,128)S(1)} %pad_maximum_fusion.1.chip_mis), custom_call_target="tpu_custom_call" | custom-call | flops 6553600 | bytes 524288 | tf_op jit(solution)/shard_map/adjoint_chip/pallas_call | solution.py:379
  46.7 0.3 slopes.1
  47.0 4.4 %collective-permute-done.3.prior_ends = f32[4,4,64,128]{3,2,1,0:T(8,128)S(1)} collective-permute-done((f32[4,4,64,128]{3,2,1,0:T(8,128)S(1)}, f32[4,4,64,128]{3,2,1,0:T(8,128)S(1)}, u32[]{:S(2)}, u32[]{:S(2)}) %collective-permute-start.3) | collective-permute-done | bytes 524320 | tf_op jit(solution)/shard_map/ppermute | solution.py:372
  51.4 0.2 carry.1.prior
  51.6 0.0 collective-permute-done.2.cross_mis
  51.6 2.0 %adjoint_cross.1 = f32[4,4,64,128]{3,2,1,0:T(8,128)} custom-call(f32[1]{0:T(128)S(6)} %copy.6.step_size, f32[4,4,64,128]{3,2,1,0:T(8,128)S(1)} %stage.1.own, f32[4,4,64,128]{3,2,1,0:T(8,128)S(1)} %pad_maximum_fusion.chip, f32[4,4,64,128]{3,2,1,0:T(8,128)S(1)} %collective-permute-done.cross, f32[4,4,64,128]{3,2,1,0:T(8,128)S(1)} %compare.2.own_mis.source, ...), custom_call_target="tpu_custom_call" | custom-call | flops 6553600 | bytes 524288 | tf_op jit(solution)/shard_map/adjoint_cross/pallas_call | solution.py:382
  (8 shorter events, 0.2 us)
Async XLA Ops:
  0.6 24.7 %copy-start = (f32[1,4,4,64,128]{4,3,2,1,0:T(8,128)S(1)}, f32[1,4,4,64,128]{4,3,2,1,0:T(8,128)}, u32[]{:S(2)}) copy-start(f32[1,4,4,64,128]{4,3,2,1,0:T(8,128)} %param.3) | copy-start | bytes 1572868
  0.6 27.0 %collective-permute-start = (f32[4,4,64,128]{3,2,1,0:T(8,128)}, f32[4,4,64,128]{3,2,1,0:T(8,128)S(1)}, u32[]{:S(2)}, u32[]{:S(2)}) collective-permute-start(f32[4,4,64,128]{3,2,1,0:T(8,128)} %bitcast.13), channel_id=1, source_target_pairs={{0,31},{1,2},{2,1},{3,4},{4,3},{5,6},{6,5},{7,8},{8,7},{9,10},{10,... | collective-permute-start | bytes 1572872 | tf_op jit(solution)/shard_map/ppermute | solution.py:361
  6.2 23.7 %collective-permute-start.1 = (f32[4,4,64,128]{3,2,1,0:T(8,128)}, f32[4,4,64,128]{3,2,1,0:T(8,128)S(1)}, u32[]{:S(2)}, u32[]{:S(2)}) collective-permute-start(f32[4,4,64,128]{3,2,1,0:T(8,128)} %bitcast.14), channel_id=1, source_target_pairs={{32,0},{64,32},{96,64},{128,96},{160,128},{192,160},{224,192},{256... | collective-permute-start | bytes 1572872 | tf_op jit(solution)/shard_map/ppermute | solution.py:367
  29.9 21.5 %collective-permute-start.3 = (f32[4,4,64,128]{3,2,1,0:T(8,128)S(1)}, f32[4,4,64,128]{3,2,1,0:T(8,128)S(1)}, u32[]{:S(2)}, u32[]{:S(2)}) collective-permute-start(f32[4,4,64,128]{3,2,1,0:T(8,128)S(1)} %forward_chip.1.ends), channel_id=1, source_target_pairs={{0,32},{32,64},{64,96},{96,128},{128,160},{160,192},{192,224},{224... | collective-permute-start | bytes 1572872 | tf_op jit(solution)/shard_map/ppermute | solution.py:372
  32.1 19.5 %collective-permute-start.2 = (f32[4,4,64,128]{3,2,1,0:T(8,128)S(1)}, f32[4,4,64,128]{3,2,1,0:T(8,128)S(1)}, u32[]{:S(2)}, u32[]{:S(2)}) collective-permute-start(f32[4,4,64,128]{3,2,1,0:T(8,128)S(1)} %compare.2.own_mis.source), channel_id=1, source_target_pairs={{0,31},{1,2},{2,1},{3,4},{4,3},{5,6},{6,5},{7,8},{8,7},{9,10},{10,... | collective-permute-start | bytes 1572872 | tf_op jit(solution)/shard_map/ppermute | solution.py:374
